TPU v7x, 1024 devices: a whole 8x8x8 slice. The times are simulated.
1024 devices in a mesh: vel: 16 (over y_lo, x), space: 64 (over y_hi, z, core).
Axes of the slice: x: 8, y: 8 (y_hi: 4, y_lo: 2; y = y_hi * 2 + y_lo), z: 8, core: 2. Of those that a mesh axis runs over, the one named last changes fastest.
Arguments:
- distribution: float32 [2304, 256, 256], P('vel', 'space'), may hold values from -3 to 3
- moments_old: float32 [10, 256, 256], P(None, 'space'), may hold values from -6 to 6
- pore_mask: int32 [256, 256], P('space'), may hold values 0 or 1
- synthetic_rate: float32 [10], replicated, may hold values from 0.2 to 4
Outputs:
- distribution_new: float32 [2304, 256, 256], P('vel', 'space')
- moments_new: float32 [10, 256, 256], P(None, 'space')
Inputs may be any that keep to these rules, and one draw needn't show every extreme that they name: `pore_mask`: 1 marks a pore cell, 0 a solid one.
All inputs are finite; a program needn't handle non-finite values. No bound on the sum of `pore_mask` on one device may be relied on, other than what follows from the above.
Results may differ from a plain program's by a relative error of at most 0.000092.
Values sent between devices are 32-bit elements; how exact they have to be, the bound alone decides.
No kernel may reach another device: no remote copies, remote signals or barrier semaphores. Data moves between devices by JAX's collectives and lax.ppermute only.
A program may use at most 32 MiB of HBM per device.

v0:
```python
import math

import jax
import jax.numpy as jnp
from jax import lax
from jax.experimental import pallas as pl
from jax.experimental.pallas import tpu as pltpu
from jax.sharding import PartitionSpec as P


F = jnp.float32
SHAPE = (8, 128)
VOL = 216.0 / 2304 / math.pi**1.5
K1, K4, K5 = 2.0, 0.6667, 0.8


def magnitude(kk):
    return 2.75 - 0.5 * kk


def iotas():
    return lax.broadcasted_iota(jnp.int32, SHAPE, 0), lax.broadcasted_iota(jnp.int32, SHAPE, 1)


def first_speed(i_ref):
    return jnp.full(SHAPE, -3.0 + (i_ref[0].astype(F) + 0.5) * 0.375, F)


def field_polynomial(a, m):
    a2 = a * a
    u, w = a2 - 1.5, a2 - 2.5
    return (
        m[0] + K1 * (a * m[1]) + K4 * (u * m[4]) + K5 * (a * w * m[5]),
        K1 * m[2] + K5 * (w * m[6]) + K1 * (a * m[8]),
        K1 * m[3] + K5 * (w * m[7]),
        K4 * m[4] + K5 * (a * m[5]),
        K5 * m[6],
        K5 * m[7],
        K1 * m[9],
    )


def at_second(al, b):
    b2 = b * b
    return (
        al[0] + b * al[1] + b2 * al[3] + (b2 * b) * al[4],
        al[2] + b2 * al[5] + b * al[6],
        al[3] + b * al[4],
        al[5],
    )


def from_z(h, lane, positive):
    inside = lane & 15
    if positive:
        return jnp.where(inside == 0, pltpu.roll(h, 113, 1), pltpu.roll(h, 1, 1))
    return jnp.where(inside == 15, pltpu.roll(h, 15, 1), pltpu.roll(h, 127, 1))


def from_y(h, lane, positive, swap):
    r = pltpu.roll(h, 16 if positive else 112, 1)
    return jnp.where(lane < 16 if positive else lane >= 112, swap(r), r)


def swap_halves(r):
    return pltpu.roll(r, 4, 0)


def swap_pairs(r):
    even = (lax.broadcasted_iota(jnp.int32, SHAPE, 0) & 1) == 0
    return jnp.where(even, pltpu.roll(r, 7, 0), pltpu.roll(r, 1, 0))


def add_raw(sums, b, acc):
    s0, sb, sc, s2, sb2, sc2, sbc = sums
    p, q, r, t = acc
    b2 = b * b
    return (
        s0 + p,
        sb + b * p,
        sc + q,
        s2 + b2 * p + r,
        sb2 + b * (b2 * p + r),
        sc2 + b2 * q + t,
        sbc + b * q,
    )


def pack_kernel(i_ref, x_hbm, m_hbm, p_hbm, g_ref, o_ref, x_ref, m_ref, p_ref, sem):
    copies = [
        pltpu.make_async_copy(src, dst, sem.at[n])
        for n, (src, dst) in enumerate(((x_hbm, x_ref), (m_hbm, m_ref), (p_hbm, p_ref)))
    ]
    for copy in copies:
        copy.start()
    a = first_speed(i_ref)
    aa = jnp.abs(a)
    sub, lane = iotas()
    even_row = (sub & 1) == 0
    zero = jnp.zeros(SHAPE, F)
    cs = [-2.75 + 0.5 * (4 * t + (sub >> 1)).astype(F) for t in range(3)]
    ecs = [jnp.exp(-c * c) for c in cs]
    for copy in copies:
        copy.wait()

    def back(h, t):
        if t == 0:
            return from_z(h, lane, False)
        if t == 2:
            return from_z(h, lane, True)
        return jnp.where(sub < 4, from_z(h, lane, False), from_z(h, lane, True))

    def build(near, far):
        o_ref[0:288, :] = x_ref[pl.ds(near, 288, stride=4), :]
        o_ref[288:576, :] = x_ref[pl.ds(far, 288, stride=4), :]
        o_ref[576:596, :] = m_ref[pl.ds(near, 20, stride=4), :]
        o_ref[596:598, :] = p_ref[pl.ds(near, 2, stride=4), :].astype(F)
        o_ref[598:600, :] = jnp.zeros((2, 128), F)

        def pair(r):
            return jnp.where(
                even_row,
                jnp.broadcast_to(o_ref[r : r + 1, :], SHAPE),
                jnp.broadcast_to(o_ref[r + 1 : r + 2, :], SHAPE),
            )

        pore = pair(596)
        al = field_polynomial(a, [pair(576 + 2 * m) for m in range(10)])

        def step(jj, carry):
            whole, down, up, minus, plus, double = carry
            bm = 2.75 - 0.5 * jj.astype(F)
            ex = jnp.exp(-(a * a) - bm * bm)
            polys = [at_second(al, -bm), at_second(al, bm)]
            outs = [[zero] * 4, [zero] * 4]
            powers = [[[zero] * 5] * 3, [[zero] * 5] * 3]
            for t in range(3):
                c = cs[t]
                ca = jnp.abs(c)
                r = 1.0 / (aa + ca + (1.0 + bm))
                wa, wb, wc = aa * r, bm * r, ca * r
                rg = r * ex * ecs[t]
                for side in range(2):
                    p0, p1, p2, p3 = polys[side]
                    g = rg * (p0 + c * (p1 + c * (p2 + c * p3)))
                    base = pl.multiple_of(((11 - jj) if side else jj) * 24 + 8 * t, 8)
                    f1, f2 = o_ref[pl.ds(base, 8), :], o_ref[pl.ds(288 + base, 8), :]
                    h = (wa * pore) * (
                        g + wa * f2 + wb * from_y(f1, lane, side == 1, swap_pairs) + wc * back(f1, t)
                    )
                    k = wa * r * f1
                    ks, hs = [k], [h]
                    for _ in range(4):
                        ks.append(c * ks[-1])
                    for _ in range(3):
                        hs.append(c * hs[-1])
                    powers[side] = powers[side][:t] + [ks] + powers[side][t + 1 :]
                    outs[side] = [p + q for p, q in zip(outs[side], hs)]
            sides = [down, up]
            for side in range(2):
                b = bm if side else -bm
                low, mid, high = powers[side]
                total = [low[n] + mid[n] + high[n] for n in range(4)]
                sides[side] = add_raw(sides[side], b, [bm * x for x in total])
                double = add_raw(double, b, total)
                minus = add_raw(minus, b, [low[n] + jnp.where(sub < 4, mid[n], 0.0) for n in range(1, 5)])
                plus = add_raw(plus, b, [high[n] + jnp.where(sub < 4, 0.0, mid[n]) for n in range(1, 5)])
                whole = add_raw(whole, b, outs[side])
            return whole, sides[0], sides[1], minus, plus, double

        groups = lax.fori_loop(0, 6, step, ((zero,) * 7,) * 6)
        scale = (1.0, 1.0, 1.0, -1.0, 1.0, aa)
        for n in range(6):
            for m in range(7):
                x = groups[n][m]
                x = x + pltpu.roll(x, 2, 0)
                x = (x + pltpu.roll(x, 4, 0)) * scale[n]
                g_ref[16 * n + 2 * m : 16 * n + 2 * m + 2, :] = x[0:2, :]
            g_ref[16 * n + 14 : 16 * n + 16, :] = jnp.zeros((2, 128), F)

    pl.when(i_ref[0] >= 8)(lambda: build(3, 2))
    pl.when(i_ref[0] < 8)(lambda: build(0, 1))


def local_kernel(i_ref, r_ref, x_ref, m_ref, p_ref, h_ref, s_ref, q_ref):
    for m in range(10):
        q_ref[m] = 1.0 / (jnp.full(SHAPE, r_ref[m], F) + 6.0)
    a = first_speed(i_ref)
    aa = jnp.abs(a)
    sub, lane = iotas()
    pore = p_ref[...].astype(F)
    al = field_polynomial(a, [m_ref[m] for m in range(10)])
    zero = jnp.zeros(SHAPE, F)

    def sweeps(shift, edge):
        inner = jnp.where((sub & 3) == edge, 0.0, 1.0)

        def step(jj, sums):
            bm = 2.75 - 0.5 * jj.astype(F)
            ex = jnp.exp(-(a * a) - bm * bm)
            accs = [[zero] * 4, [zero] * 4]
            polys = [at_second(al, -bm), at_second(al, bm)]
            rows = [jj * 12, (11 - jj) * 12]
            for kk in range(6):
                cm = magnitude(kk)
                c2 = cm * cm
                pr = pore * (1.0 / (aa + (1.0 + cm + bm)))
                pg = pr * (ex * math.exp(-c2))
                px, py, pz = aa * pr * inner, bm * pr, cm * pr
                for side in range(2):
                    p0, p1, p2, p3 = polys[side]
                    even, odd = p0 + c2 * p2, cm * (p1 + c2 * p3)
                    out = []
                    for up in range(2):
                        v = rows[side] + (11 - kk if up else kk)
                        g = pg * (even + odd if up else even - odd)
                        h = x_ref[v]
                        for _ in range(2):
                            h = (
                                g
                                + px * pltpu.roll(h, shift, 0)
                                + py * from_y(h, lane, side == 1, swap_halves)
                                + pz * from_z(h, lane, up == 1)
                            )
                        h_ref[v] = h
                        out.append(h)
                    s, d = out[1] + out[0], cm * (out[1] - out[0])
                    p, q, r, t = accs[side]
                    accs[side] = [p + s, q + d, r + c2 * s, t + c2 * d]
            sums = add_raw(sums, -bm, accs[0])
            return add_raw(sums, bm, accs[1])

        sums = lax.fori_loop(0, 6, step, (zero,) * 7)
        for n in range(7):
            s_ref[n] = sums[n]

    pl.when(i_ref[0] >= 8)(lambda: sweeps(1, 0))
    pl.when(i_ref[0] < 8)(lambda: sweeps(7, 3))


def merge_kernel(i_ref, g_ref, p_ref, s_ref, o_ref, e_ref):
    a = first_speed(i_ref)
    sub, lane = iotas()
    even_row = (sub & 1) == 0
    forward = i_ref[0] >= 8

    def row(ref, r):
        return jnp.broadcast_to(ref[r : r + 1, :].astype(F), SHAPE)

    def own(plus, minus):
        return jnp.where(
            even_row,
            jnp.where(forward, row(p_ref, plus), row(p_ref, minus)),
            jnp.where(forward, row(p_ref, plus + 4), row(p_ref, minus + 4)),
        )

    pore_0, pore_1 = own(0, 3), own(1, 2)
    for n in range(2):
        whole, down, up, minus, plus, double = [g_ref[16 * k + 8 * n : 16 * k + 8 * n + 8, :] for k in range(6)]
        e_ref[8 * n : 8 * n + 8, :] = pore_0 * (
            whole
            + from_y(pore_0 * down, lane, False, swap_pairs)
            + from_y(pore_0 * up, lane, True, swap_pairs)
            + from_z(pore_0 * minus, lane, False)
            + from_z(pore_0 * plus, lane, True)
        )
        e_ref[16 + 8 * n : 24 + 8 * n, :] = pore_0 * pore_1 * double
    place = sub & 3
    at_near = place == jnp.where(forward, 0, 3)
    at_far = place == jnp.where(forward, 1, 2)

    def spread(r):
        return jnp.where(sub < 4, row(e_ref, r), row(e_ref, r + 1))

    s0, sb, sc, s2, sb2, sc2, sbc = [
        s_ref[n] + jnp.where(at_near, spread(2 * n), jnp.where(at_far, spread(16 + 2 * n), 0.0))
        for n in range(7)
    ]
    a2 = a * a
    t4, t5 = (a2 - 1.5) * s0 + s2, (a2 - 2.5) * s0 + s2
    moments = (s0, a * s0, sb, sc, t4, a * t5, (a2 - 2.5) * sb + sb2, (a2 - 2.5) * sc + sc2, a * sb, sbc)
    for m in range(10):
        value = moments[m] * VOL
        for n in range(o_ref.shape[0]):
            o_ref[n, 8 * m : 8 * m + 8, :] = value


def total_kernel(g_ref, o_ref):
    total = (g_ref[0] + g_ref[1]) + (g_ref[2] + g_ref[3])
    for n in range(o_ref.shape[0]):
        o_ref[n] = total


def change_kernel(g_ref, m_ref, p_ref, o_ref, h_ref):
    total = (g_ref[0] + g_ref[1]) + (g_ref[2] + g_ref[3])
    h_ref[...] = total
    o_ref[0:80, :] = total - m_ref[...]
    o_ref[80:88, :] = p_ref[...].astype(F)


def halo_kernel(i_ref, g_ref, p_ref, h_ref, o_ref):
    a = first_speed(i_ref)
    aa = jnp.abs(a)
    sub, lane = iotas()
    even_row = (sub & 1) == 0

    def row(ref, r):
        return jnp.broadcast_to(ref[r : r + 1, :].astype(F), SHAPE)

    def pair(ref, r, s):
        return jnp.where(even_row, row(ref, r), row(ref, s))

    cs = [-2.75 + 0.5 * (4 * t + (sub >> 1)).astype(F) for t in range(3)]
    ecs = [jnp.exp(-c * c) for c in cs]
    pore_out = pair(g_ref, 596, 597)
    al = field_polynomial(a, [pair(g_ref, 576 + 2 * m, 577 + 2 * m) for m in range(10)])
    o_ref[...] = h_ref[...]

    def back(h, t):
        if t == 0:
            return from_z(h, lane, False)
        if t == 2:
            return from_z(h, lane, True)
        return jnp.where(sub < 4, from_z(h, lane, False), from_z(h, lane, True))

    def fix(at_0, at_1):
        pore_0, pore_1 = pair(p_ref, at_0, at_0 + 4), pair(p_ref, at_1, at_1 + 4)

        def step(jj, carry):
            bm = 2.75 - 0.5 * jj.astype(F)
            ex = jnp.exp(-(a * a) - bm * bm)
            polys = [at_second(al, -bm), at_second(al, bm)]
            for t in range(3):
                c = cs[t]
                ca = jnp.abs(c)
                r = 1.0 / (aa + ca + (1.0 + bm))
                wa, wb, wc = aa * r, bm * r, ca * r
                rg = r * ex * ecs[t]
                for side in range(2):
                    p0, p1, p2, p3 = polys[side]
                    g = rg * (p0 + c * (p1 + c * (p2 + c * p3)))
                    base = pl.multiple_of(((11 - jj) if side else jj) * 24 + 8 * t, 8)
                    near, far = g_ref[pl.ds(base, 8), :], g_ref[pl.ds(288 + base, 8), :]
                    outer = pore_out * (
                        g + wa * far + wb * from_y(near, lane, side == 1, swap_pairs) + wc * back(near, t)
                    )
                    first = pore_0 * wa * near
                    e0 = pore_0 * (
                        wa * outer + wb * from_y(first, lane, side == 1, swap_pairs) + wc * back(first, t)
                    )
                    e1 = pore_1 * wa * first
                    rows_0 = pl.ds(base * 4 + at_0, 8, stride=4)
                    rows_1 = pl.ds(base * 4 + at_1, 8, stride=4)
                    o_ref[rows_0, :] = o_ref[rows_0, :] + e0
                    o_ref[rows_1, :] = o_ref[rows_1, :] + e1
            return carry

        lax.fori_loop(0, 6, step, 0)

    pl.when(i_ref[0] >= 8)(lambda: fix(0, 1))
    pl.when(i_ref[0] < 8)(lambda: fix(3, 2))


def final_kernel(i_ref, q_ref, h_ref, c_ref, left_ref, right_ref, mh_ref, o_hbm, mo_ref, k_ref, o_ref, sem):
    a = first_speed(i_ref)
    sub, lane = iotas()
    pores = [left_ref[10], c_ref[10], right_ref[10]]
    low, high = (sub & 3) == 0, (sub & 3) == 3
    wrap_up, wrap_down = lane < 16, lane >= 112

    def around(h):
        up, down = pltpu.roll(h, 16, 1), pltpu.roll(h, 112, 1)
        same = jnp.where(wrap_up, 0.0, up) + jnp.where(wrap_down, 0.0, down)
        other = jnp.where(wrap_up, up, jnp.where(wrap_down, down, 0.0))
        return same + swap_halves(other) + from_z(h, lane, True) + from_z(h, lane, False)

    for m in range(10):
        inv = q_ref[m]
        q = [p * inv for p in pores]
        change = [left_ref[m], c_ref[m], right_ref[m]]
        cor = [q[n] * change[n] for n in range(3)]
        for it in range(4):
            new = list(cor)
            for n in range(3):
                if it == 3 and n != 1:
                    continue
                below = pltpu.roll(cor[n], 1, 0)
                above = pltpu.roll(cor[n], 7, 0)
                if n > 0:
                    below = jnp.where(low, pltpu.roll(cor[n - 1], 5, 0), below)
                if n < 2:
                    above = jnp.where(high, pltpu.roll(cor[n + 1], 3, 0), above)
                new[n] = q[n] * (change[n] + (below + above + around(cor[n])))
            cor = new
        k_ref[m] = cor[1]
        mo_ref[m] = mh_ref[m] + cor[1]

    al = field_polynomial(a, [k_ref[m] for m in range(10)])
    pore = pores[1]

    def chunk(n, j):
        rows = pl.ds(j * 12, 12)
        return pltpu.make_async_copy(o_ref.at[rows], o_hbm.at[rows], sem.at[n])

    def step(jj, carry):
        bm = 2.75 - 0.5 * jj.astype(F)
        ex = pore * jnp.exp(-(a * a) - bm * bm)
        for side in range(2):
            p0, p1, p2, p3 = at_second(al, bm if side else -bm)
            j = 11 - jj if side else jj
            for kk in range(6):
                cm = magnitude(kk)
                c2 = cm * cm
                w = ex * math.exp(-c2)
                even, odd = w * (p0 + c2 * p2), w * (cm * (p1 + c2 * p3))
                for up in range(2):
                    v = j * 12 + (11 - kk if up else kk)
                    o_ref[v] = h_ref[v] + (even + odd if up else even - odd)
            chunk(6 * side + jj, j).start()
        return carry

    lax.fori_loop(0, 6, step, 0)
    for jj in range(6):
        chunk(jj, jj).wait()
        chunk(6 + jj, 11 - jj).wait()


VM = pl.BlockSpec(memory_space=pltpu.VMEM)
SM = pl.BlockSpec(memory_space=pltpu.SMEM)
HBM = pl.BlockSpec(memory_space=pltpu.HBM)


def call(kernel, outs, args, cost, scratch=(), ins=None, out_specs=None, grant=4 << 20):
    shapes = [jax.ShapeDtypeStruct(s, F) for s in outs]
    out_specs = out_specs or [VM] * len(shapes)
    single = len(shapes) == 1
    return pl.pallas_call(
        kernel,
        out_shape=shapes[0] if single else shapes,
        in_specs=ins,
        out_specs=out_specs[0] if single else out_specs,
        scratch_shapes=list(scratch),
        compiler_params=pltpu.CompilerParams(vmem_limit_bytes=grant),
        cost_estimate=pl.CostEstimate(flops=cost, bytes_accessed=4 * cost, transcendentals=0),
    )(*args)


def to_registers(x):
    n = x.shape[0]
    return x.reshape(n, 4, 2, 128).transpose(0, 2, 1, 3).reshape(n, 8, 128)


def from_registers(x):
    n = x.shape[0]
    return x.reshape(n, 2, 4, 128).transpose(0, 2, 1, 3).reshape(n, 4, 256)


def groups_of(key):
    found = {}
    for v in range(16):
        found.setdefault(key(v), []).append(v)
    return list(found.values())


FAR = groups_of(lambda v: (v // 8, v % 2))
NEAR = groups_of(lambda v: (v % 8) // 2)


def upwind_pairs(space):
    return [
        (v * space + s, v * space + (s + (1 if v >= 8 else -1)) % space) for v in range(16) for s in range(space)
    ]


def body(distribution, moments_old, pore_mask, synthetic_rate):
    space = lax.axis_size("space")
    i = lax.axis_index("vel").astype(jnp.int32).reshape(1)
    x = to_registers(distribution)
    old = to_registers(moments_old)
    pore = to_registers(pore_mask[None])[0]
    packed, planes = call(
        pack_kernel,
        [(96, 128), (600, 128)],
        [i, x.reshape(1152, 128), old.reshape(80, 128), pore],
        1 << 20,
        [
            pltpu.VMEM((1152, 128), F),
            pltpu.VMEM((80, 128), F),
            pltpu.VMEM((8, 128), jnp.int32),
            pltpu.SemaphoreType.DMA((3,)),
        ],
        [SM, HBM, HBM, HBM],
        grant=60 << 20,
    )
    pairs = upwind_pairs(space)
    sums_in = lax.ppermute(packed, ("vel", "space"), pairs)
    planes_in = lax.ppermute(planes, ("vel", "space"), pairs)
    half, sums, inverse = call(
        local_kernel,
        [(144, 8, 128), (7, 8, 128), (10, 8, 128)],
        [i, synthetic_rate, x, old, pore],
        1 << 21,
        ins=[SM, SM, VM, VM, VM],
    )
    copies = call(
        merge_kernel,
        [(4, 80, 128)],
        [i, sums_in, pore, sums],
        1 << 16,
        [pltpu.VMEM((32, 128), F)],
        ins=[SM, VM, VM, VM],
    )
    got = lax.all_to_all(copies, "vel", 0, 0, axis_index_groups=FAR, tiled=True)
    copies = call(total_kernel, [(4, 80, 128)], [got], 1 << 16, ins=[VM])
    got = lax.all_to_all(copies, "vel", 0, 0, axis_index_groups=NEAR, tiled=True)
    message, moments_half = call(
        change_kernel, [(88, 128), (80, 128)], [got, old.reshape(80, 128), pore], 1 << 16, ins=[VM] * 3
    )
    ring = [(s, (s + 1) % space) for s in range(space)]
    left = lax.ppermute(message, "space", ring)
    right = lax.ppermute(message, "space", [(t, s) for s, t in ring])
    whole = call(
        halo_kernel,
        [(1152, 128)],
        [i, planes_in, pore, half.reshape(1152, 128)],
        1 << 20,
        ins=[SM, VM, VM, VM],
    )
    out, moments_new = call(
        final_kernel,
        [(144, 8, 128), (10, 8, 128)],
        [
            i,
            inverse,
            whole.reshape(144, 8, 128),
            message.reshape(11, 8, 128),
            left.reshape(11, 8, 128),
            right.reshape(11, 8, 128),
            moments_half.reshape(10, 8, 128),
        ],
        1 << 20,
        [pltpu.VMEM((10, 8, 128), F), pltpu.VMEM((144, 8, 128), F), pltpu.SemaphoreType.DMA((12,))],
        [SM] + [VM] * 6,
        [HBM, VM],
    )
    return from_registers(out), from_registers(moments_new)


def solution(mesh):
    placed = (P("vel", "space", None), P(None, "space", None), P("space", None), P())
    return jax.shard_map(
        body,
        mesh=mesh,
        in_specs=placed,
        out_specs=(P("vel", "space", None), P(None, "space", None)),
        check_vma=False,
    )
```

profile of v0, /device:TPU:2, one launch (start us, length us, event | category | flops | bytes accessed | tf_op | source)
XLA Modules:
  0.0 67.8 jit_solution(1962698825323486302)
XLA Ops:
  0.6 0.0 copy-start
  0.6 0.0 copy-start.1
  0.7 2.6 %shard_map.60 = (f32[96,128]{1,0:T(8,128)}, f32[600,128]{1,0:T(8,128)}) custom-call(s32[1]{0:T(128)} %bitcast.i_ref, f32[1152,128]{1,0:T(8,128)} %bitcast.36, f32[80,128]{1,0:T(8,128)} %bitcast.40, s32[8,128]{1,0:T(8,128)} %bitcast.43), custom_call_target="tpu_custom_call" | custom-call | flops 1048576 | bytes 4194304 | tf_op jit(solution)/shard_map/pallas_call | solution.py:437
  3.3 0.0 copy-start.2
  3.3 21.1 %collective-permute-start.1 = (f32[96,128]{1,0:T(8,128)}, f32[96,128]{1,0:T(8,128)S(1)}, u32[]{:S(2)}, u32[]{:S(2)}) collective-permute-start(f32[96,128]{1,0:T(8,128)} %get-tuple-element.14), channel_id=1, source_target_pairs={{0,63},{1,0},{2,1},{3,2},{4,3},{5,4},{6,5},{7,6},{8,7},{9,8},{10,9... | collective-permute-start | bytes 147464 | tf_op jit(solution)/shard_map/ppermute | solution.py:496
  24.4 0.0 copy-start.3
  24.4 0.0 copy-done
  24.4 0.0 copy-done.1
  24.5 0.6 copy-done.3
  25.1 2.5 %shard_map.59 = (f32[144,8,128]{2,1,0:T(8,128)S(1)}, f32[7,8,128]{2,1,0:T(8,128)S(1)}, f32[10,8,128]{2,1,0:T(8,128)S(1)}) custom-call(s32[1]{0:T(128)} %bitcast.i_ref, f32[10]{0:T(128)S(1)} %copy-done.3, f32[144,8,128]{2,1,0:T(8,128)S(1)} %bitcast.37, f32[10,8,128]{2,1,0:T(8,128)S(1)} %bitcast.41, s32[8,128]{1,0:T(8,128)S(1)} %bitcast.44), custom_call_target="tpu_custom_call" | custom-call | flops 2097152 | bytes 8388608 | tf_op jit(solution)/shard_map/pallas_call | solution.py:437
  27.6 0.0 copy-start.4
  27.6 0.0 collective-permute-done.1.g_ref
  27.6 0.8 %shard_map.62 = f32[4,80,128]{2,1,0:T(8,128)} custom-call(s32[1]{0:T(128)} %bitcast.i_ref, f32[96,128]{1,0:T(8,128)S(1)} %collective-permute-done.1.g_ref, s32[8,128]{1,0:T(8,128)S(1)} %bitcast.45, f32[7,8,128]{2,1,0:T(8,128)S(1)} %get-tuple-element.15.s_ref), custom_call_target="tpu_custom_call" | custom-call | flops 65536 | bytes 262144 | tf_op jit(solution)/shard_map/pallas_call | solution.py:437
  28.4 5.9 %all-to-all-start = ((f32[4,80,128]{2,1,0:T(8,128)}), f32[4,80,128]{2,1,0:T(8,128)S(1)}, u32[]{:S(2)}, u32[]{:S(2)}) async-start(f32[4,80,128]{2,1,0:T(8,128)} %shard_map.62), calls=%async_computation | async-start | bytes 327680 | tf_op jit(solution)/shard_map/all_to_all | solution.py:513
  34.3 6.3 %collective-permute-start = (f32[600,128]{1,0:T(8,128)S(1)}, f32[600,128]{1,0:T(8,128)S(1)}, u32[]{:S(2)}, u32[]{:S(2)}) collective-permute-start(f32[600,128]{1,0:T(8,128)S(1)} %copy-done.4), channel_id=1, source_target_pairs={{0,63},{1,0},{2,1},{3,2},{4,3},{5,4},{6,5},{7,6},{8,7},{9,8},{10,9... | collective-permute-start | bytes 921608 | tf_op jit(solution)/shard_map/ppermute | solution.py:497
  40.6 3.1 %all-to-all-done.g_ref = f32[4,80,128]{2,1,0:T(8,128)S(1)} async-done(((f32[4,80,128]{2,1,0:T(8,128)}), f32[4,80,128]{2,1,0:T(8,128)S(1)}, u32[]{:S(2)}, u32[]{:S(2)}) %all-to-all-start) | async-done | bytes 163872 | tf_op jit(solution)/shard_map/all_to_all | solution.py:513
  43.7 7.5 %all_to_all.10.g_ref = f32[4,80,128]{2,1,0:T(8,128)S(1)} all-to-all(f32[4,80,128]{2,1,0:T(8,128)S(1)} %shard_map.63), channel_id=1, replica_groups={{0,64,512,576},{128,192,640,704},{256,320,768,832},{384,448,896,960},{1..., dimensions={0} | all-to-all | bytes 327680 | tf_op jit(solution)/shard_map/all_to_all | solution.py:515
  51.2 3.8 %collective-permute-start.3 = (f32[88,128]{1,0:T(8,128)S(1)}, f32[88,128]{1,0:T(8,128)S(1)}, u32[]{:S(2)}, u32[]{:S(2)}) collective-permute-start(f32[88,128]{1,0:T(8,128)S(1)} %get-tuple-element.16), channel_id=1, source_target_pairs={{1,0},{2,1},{3,2},{4,3},{5,4},{6,5},{7,6},{8,7},{9,8},{10,9},{11,1... | collective-permute-start | bytes 135176 | tf_op jit(solution)/shard_map/ppermute | solution.py:521
  54.9 1.9 %collective-permute-start.2 = (f32[88,128]{1,0:T(8,128)S(1)}, f32[88,128]{1,0:T(8,128)S(1)}, u32[]{:S(2)}, u32[]{:S(2)}) collective-permute-start(f32[88,128]{1,0:T(8,128)S(1)} %get-tuple-element.16), channel_id=1, source_target_pairs={{0,1},{1,2},{2,3},{3,4},{4,5},{5,6},{6,7},{7,8},{8,9},{9,10},{10,1... | collective-permute-start | bytes 135176 | tf_op jit(solution)/shard_map/ppermute | solution.py:520
  56.9 0.0 collective-permute-done.g_ref
  56.9 0.8 %shard_map.61 = f32[1152,128]{1,0:T(8,128)S(1)} custom-call(s32[1]{0:T(128)} %bitcast.i_ref, f32[600,128]{1,0:T(8,128)S(1)} %collective-permute-done.g_ref, s32[8,128]{1,0:T(8,128)S(1)} %bitcast.47, f32[1152,128]{1,0:T(8,128)S(1)} %bitcast.39), custom_call_target="tpu_custom_call" | custom-call | flops 1048576 | bytes 4194304 | tf_op jit(solution)/shard_map/pallas_call | solution.py:437
  57.7 0.0 collective-permute-done.3
  57.7 6.8 %collective-permute-done.2 = f32[88,128]{1,0:T(8,128)S(1)} collective-permute-done((f32[88,128]{1,0:T(8,128)S(1)}, f32[88,128]{1,0:T(8,128)S(1)}, u32[]{:S(2)}, u32[]{:S(2)}) %collective-permute-start.2) | collective-permute-done | bytes 45088 | tf_op jit(solution)/shard_map/ppermute | solution.py:520
  64.5 3.3 %shard_map.65 = (f32[144,8,128]{2,1,0:T(8,128)}, f32[10,8,128]{2,1,0:T(8,128)}) custom-call(s32[1]{0:T(128)} %bitcast.i_ref, f32[10,8,128]{2,1,0:T(8,128)S(1)} %get-tuple-element.11.q_ref, f32[144,8,128]{2,1,0:T(8,128)S(1)} %bitcast.38, f32[11,8,128]{2,1,0:T(8,128)S(1)} %bitcast.48, f32[11,8,128]{2,1,0:T(8,128)S(1)} %bitcast.50, f32[11,8,128]{2,1,0:T(8,128)S(1)} %bitcast.49, ...), custom_call_target="tpu_custom_call" | custom-call | flops 1048576 | bytes 4194304 | tf_op jit(solution)/shard_map/pallas_call | solution.py:437
  (4 shorter events, 0.0 us)
Async XLA Ops:
  0.6 23.8 %copy-start = (f32[144,4,256]{2,1,0:T(4,128)S(1)}, f32[144,4,256]{2,1,0:T(4,128)}, u32[]{:S(2)}) copy-start(f32[144,4,256]{2,1,0:T(4,128)} %param.4) | copy-start | bytes 1769476
  0.6 23.8 %copy-start.1 = (f32[10,4,256]{2,1,0:T(4,128)S(1)}, f32[10,4,256]{2,1,0:T(4,128)}, u32[]{:S(2)}) copy-start(f32[10,4,256]{2,1,0:T(4,128)} %param.5) | copy-start | bytes 122884
  3.3 21.2 %copy-start.2 = (s32[4,256]{1,0:T(4,128)S(1)}, s32[4,256]{1,0:T(4,128)}, u32[]{:S(2)}) copy-start(s32[4,256]{1,0:T(4,128)} %param.6) | copy-start | bytes 12292
  3.3 24.3 %collective-permute-start.1 = (f32[96,128]{1,0:T(8,128)}, f32[96,128]{1,0:T(8,128)S(1)}, u32[]{:S(2)}, u32[]{:S(2)}) collective-permute-start(f32[96,128]{1,0:T(8,128)} %get-tuple-element.14), channel_id=1, source_target_pairs={{0,63},{1,0},{2,1},{3,2},{4,3},{5,4},{6,5},{7,6},{8,7},{9,8},{10,9... | collective-permute-start | bytes 147464 | tf_op jit(solution)/shard_map/ppermute | solution.py:496
  24.4 0.7 copy-start.3
  27.6 6.7 %copy-start.4 = (f32[600,128]{1,0:T(8,128)S(1)}, f32[600,128]{1,0:T(8,128)}, u32[]{:S(2)}) copy-start(f32[600,128]{1,0:T(8,128)} %get-tuple-element.12) | copy-start | bytes 921604
  28.4 15.3 %all-to-all-start = ((f32[4,80,128]{2,1,0:T(8,128)}), f32[4,80,128]{2,1,0:T(8,128)S(1)}, u32[]{:S(2)}, u32[]{:S(2)}) async-start(f32[4,80,128]{2,1,0:T(8,128)} %shard_map.62), calls=%async_computation | async-start | bytes 327680 | tf_op jit(solution)/shard_map/all_to_all | solution.py:513
  34.3 22.6 %collective-permute-start = (f32[600,128]{1,0:T(8,128)S(1)}, f32[600,128]{1,0:T(8,128)S(1)}, u32[]{:S(2)}, u32[]{:S(2)}) collective-permute-start(f32[600,128]{1,0:T(8,128)S(1)} %copy-done.4), channel_id=1, source_target_pairs={{0,63},{1,0},{2,1},{3,2},{4,3},{5,4},{6,5},{7,6},{8,7},{9,8},{10,9... | collective-permute-start | bytes 921608 | tf_op jit(solution)/shard_map/ppermute | solution.py:497
  51.2 6.5 %collective-permute-start.3 = (f32[88,128]{1,0:T(8,128)S(1)}, f32[88,128]{1,0:T(8,128)S(1)}, u32[]{:S(2)}, u32[]{:S(2)}) collective-permute-start(f32[88,128]{1,0:T(8,128)S(1)} %get-tuple-element.16), channel_id=1, source_target_pairs={{1,0},{2,1},{3,2},{4,3},{5,4},{6,5},{7,6},{8,7},{9,8},{10,9},{11,1... | collective-permute-start | bytes 135176 | tf_op jit(solution)/shard_map/ppermute | solution.py:521
  54.9 9.6 %collective-permute-start.2 = (f32[88,128]{1,0:T(8,128)S(1)}, f32[88,128]{1,0:T(8,128)S(1)}, u32[]{:S(2)}, u32[]{:S(2)}) collective-permute-start(f32[88,128]{1,0:T(8,128)S(1)} %get-tuple-element.16), channel_id=1, source_target_pairs={{0,1},{1,2},{2,3},{3,4},{4,5},{5,6},{6,7},{7,8},{8,9},{9,10},{10,1... | collective-permute-start | bytes 135176 | tf_op jit(solution)/shard_map/ppermute | solution.py:520
where the time goes:
time: 68.2 us; the launch traced here: 67.8 us
  starting transfers between devices  39 us (57%)
  Pallas kernels  9.99 us (15%)
  waiting for transfers between devices  9.92 us (15%)
  blocking collectives  7.45 us (11%)
  between operations  0.79 us (1%)
    ppermute x1, starting transfers between devices, body(): sums_in = lax.ppermute(packed, ('vel', 'space'), pairs)  21.1 us
    pallas_call x7, Pallas kernels, call(): pl.pallas_call(kernel, out_shape=shapes[0] if single else shapes, in_spec...  9.99 us
    all_to_all x1, blocking collectives, body(): lax.all_to_all(copies, 'vel', 0, 0, axis_index_groups=NEAR, tiled=True)  7.45 us
    ppermute x1, waiting for transfers between devices, body(): left = lax.ppermute(message, 'space', ring)  6.83 us
    ppermute x1, starting transfers between devices, body(): planes_in = lax.ppermute(planes, ('vel', 'space'), pairs)  6.32 us
    all_to_all x1, starting transfers between devices, body(): got = lax.all_to_all(copies, 'vel', 0, 0, axis_index_groups=FAR, tiled=True)  5.85 us
    ppermute x1, starting transfers between devices, body(): right = lax.ppermute(message, 'space', [(t, s) for s, t in ring])  3.76 us
    all_to_all x1, waiting for transfers between devices, body(): got = lax.all_to_all(copies, 'vel', 0, 0, axis_index_groups=FAR, tiled=True)  3.08 us
  transfers between devices with their start and end apart: 5, of which 2 were waited for; matrix products, arithmetic and copies ran while one was open for 0% of the time, Pallas kernels for 5%

commit v1 on v0

--- a/solution.py
+++ b/solution.py
@@ -86,7 +86,7 @@
     )
 
 
-def pack_kernel(i_ref, x_hbm, m_hbm, p_hbm, g_ref, o_ref, x_ref, m_ref, p_ref, sem):
+def sums_kernel(i_ref, n_ref, x_hbm, m_hbm, p_hbm, g_ref, h_hbm, s_hbm, x_ref, m_ref, p_ref, h_ref, s_ref, sem):
     copies = [
         pltpu.make_async_copy(src, dst, sem.at[n])
         for n, (src, dst) in enumerate(((x_hbm, x_ref), (m_hbm, m_ref), (p_hbm, p_ref)))
@@ -111,21 +111,15 @@
         return jnp.where(sub < 4, from_z(h, lane, False), from_z(h, lane, True))
 
     def build(near, far):
-        o_ref[0:288, :] = x_ref[pl.ds(near, 288, stride=4), :]
-        o_ref[288:576, :] = x_ref[pl.ds(far, 288, stride=4), :]
-        o_ref[576:596, :] = m_ref[pl.ds(near, 20, stride=4), :]
-        o_ref[596:598, :] = p_ref[pl.ds(near, 2, stride=4), :].astype(F)
-        o_ref[598:600, :] = jnp.zeros((2, 128), F)
-
-        def pair(r):
+        def pair(ref, r):
             return jnp.where(
                 even_row,
-                jnp.broadcast_to(o_ref[r : r + 1, :], SHAPE),
-                jnp.broadcast_to(o_ref[r + 1 : r + 2, :], SHAPE),
+                jnp.broadcast_to(ref[r : r + 1, :].astype(F), SHAPE),
+                jnp.broadcast_to(ref[r + 4 : r + 5, :].astype(F), SHAPE),
             )
 
-        pore = pair(596)
-        al = field_polynomial(a, [pair(576 + 2 * m) for m in range(10)])
+        pore = pair(p_ref, near)
+        al = field_polynomial(a, [pair(m_ref, 8 * m + near) for m in range(10)])
 
         def step(jj, carry):
             whole, down, up, minus, plus, double = carry
@@ -144,7 +138,7 @@
                     p0, p1, p2, p3 = polys[side]
                     g = rg * (p0 + c * (p1 + c * (p2 + c * p3)))
                     base = pl.multiple_of(((11 - jj) if side else jj) * 24 + 8 * t, 8)
-                    f1, f2 = o_ref[pl.ds(base, 8), :], o_ref[pl.ds(288 + base, 8), :]
+                    f1, f2 = x_ref[pl.ds(4 * base + near, 8, stride=4), :], x_ref[pl.ds(4 * base + far, 8, stride=4), :]
                     h = (wa * pore) * (
                         g + wa * f2 + wb * from_y(f1, lane, side == 1, swap_pairs) + wc * back(f1, t)
                     )
@@ -181,15 +175,54 @@
     pl.when(i_ref[0] >= 8)(lambda: build(3, 2))
     pl.when(i_ref[0] < 8)(lambda: build(0, 1))
 
-
-def local_kernel(i_ref, r_ref, x_ref, m_ref, p_ref, h_ref, s_ref, q_ref):
-    for m in range(10):
-        q_ref[m] = 1.0 / (jnp.full(SHAPE, r_ref[m], F) + 6.0)
+    @pl.when(early(n_ref))
+    def _():
+        local_sweeps(i_ref, x_ref, m_ref, p_ref, h_ref, s_ref)
+        copies = [
+            pltpu.make_async_copy(src, dst, sem.at[n]) for n, (src, dst) in enumerate(((h_ref, h_hbm), (s_ref, s_hbm)))
+        ]
+        for copy in copies:
+            copy.start()
+        for copy in copies:
+            copy.wait()
+
+
+def planes_kernel(i_ref, x_ref, m_ref, p_ref, o_ref):
+    def take(near, far):
+        o_ref[0:288, :] = x_ref[pl.ds(near, 288, stride=4), :]
+        o_ref[288:576, :] = x_ref[pl.ds(far, 288, stride=4), :]
+        o_ref[576:596, :] = m_ref[pl.ds(near, 20, stride=4), :]
+        o_ref[596:598, :] = p_ref[pl.ds(near, 2, stride=4), :].astype(F)
+        o_ref[598:600, :] = jnp.zeros((2, 128), F)
+
+    pl.when(i_ref[0] >= 8)(lambda: take(3, 2))
+    pl.when(i_ref[0] < 8)(lambda: take(0, 1))
+
+
+def late_kernel(i_ref, n_ref, x_ref, m_ref, p_ref, h_hbm, s_hbm, h_ref, s_ref, sem):
+    @pl.when(early(n_ref))
+    def _():
+        copies = [
+            pltpu.make_async_copy(src, dst, sem.at[n]) for n, (src, dst) in enumerate(((h_hbm, h_ref), (s_hbm, s_ref)))
+        ]
+        for copy in copies:
+            copy.start()
+        for copy in copies:
+            copy.wait()
+
+    pl.when(jnp.logical_not(early(n_ref)))(lambda: local_sweeps(i_ref, x_ref, m_ref, p_ref, h_ref, s_ref))
+
+
+def early(n_ref):
+    return lax.rem(n_ref[0], 16) < 4
+
+
+def local_sweeps(i_ref, x_ref, m_ref, p_ref, h_ref, s_ref):
     a = first_speed(i_ref)
     aa = jnp.abs(a)
     sub, lane = iotas()
     pore = p_ref[...].astype(F)
-    al = field_polynomial(a, [m_ref[m] for m in range(10)])
+    al = field_polynomial(a, [m_ref[8 * m : 8 * m + 8, :] for m in range(10)])
     zero = jnp.zeros(SHAPE, F)
 
     def sweeps(shift, edge):
@@ -214,7 +247,7 @@
                     for up in range(2):
                         v = rows[side] + (11 - kk if up else kk)
                         g = pg * (even + odd if up else even - odd)
-                        h = x_ref[v]
+                        h = x_ref[pl.ds(pl.multiple_of(8 * v, 8), 8), :]
                         for _ in range(2):
                             h = (
                                 g
@@ -298,7 +331,9 @@
     o_ref[80:88, :] = p_ref[...].astype(F)
 
 
-def halo_kernel(i_ref, g_ref, p_ref, h_ref, o_ref):
+def halo_kernel(i_ref, r_ref, g_ref, p_ref, h_ref, o_ref, q_ref):
+    for m in range(10):
+        q_ref[m] = 1.0 / (jnp.full(SHAPE, r_ref[m], F) + 6.0)
     a = first_speed(i_ref)
     aa = jnp.abs(a)
     sub, lane = iotas()
@@ -475,32 +510,40 @@
 def body(distribution, moments_old, pore_mask, synthetic_rate):
     space = lax.axis_size("space")
     i = lax.axis_index("vel").astype(jnp.int32).reshape(1)
+    n = lax.axis_index("space").astype(jnp.int32).reshape(1)
     x = to_registers(distribution)
     old = to_registers(moments_old)
     pore = to_registers(pore_mask[None])[0]
-    packed, planes = call(
-        pack_kernel,
-        [(96, 128), (600, 128)],
-        [i, x.reshape(1152, 128), old.reshape(80, 128), pore],
+    shapes = [(144, 8, 128), (7, 8, 128)]
+    flat = [x.reshape(1152, 128), old.reshape(80, 128), pore]
+    packed, half, sums = call(
+        sums_kernel,
+        [(96, 128)] + shapes,
+        [i, n] + flat,
         1 << 20,
         [
             pltpu.VMEM((1152, 128), F),
             pltpu.VMEM((80, 128), F),
             pltpu.VMEM((8, 128), jnp.int32),
+            pltpu.VMEM((144, 8, 128), F),
+            pltpu.VMEM((7, 8, 128), F),
             pltpu.SemaphoreType.DMA((3,)),
         ],
-        [SM, HBM, HBM, HBM],
+        [SM, SM, HBM, HBM, HBM],
+        [VM, HBM, HBM],
         grant=60 << 20,
     )
     pairs = upwind_pairs(space)
     sums_in = lax.ppermute(packed, ("vel", "space"), pairs)
+    planes = call(planes_kernel, [(600, 128)], [i] + flat, 1 << 16, ins=[SM, VM, VM, VM])
     planes_in = lax.ppermute(planes, ("vel", "space"), pairs)
-    half, sums, inverse = call(
-        local_kernel,
-        [(144, 8, 128), (7, 8, 128), (10, 8, 128)],
-        [i, synthetic_rate, x, old, pore],
+    half, sums = call(
+        late_kernel,
+        shapes,
+        [i, n] + flat + [half, sums],
         1 << 21,
-        ins=[SM, SM, VM, VM, VM],
+        [pltpu.SemaphoreType.DMA((2,))],
+        [SM, SM, VM, VM, VM, HBM, HBM],
     )
     copies = call(
         merge_kernel,
@@ -519,12 +562,12 @@
     ring = [(s, (s + 1) % space) for s in range(space)]
     left = lax.ppermute(message, "space", ring)
     right = lax.ppermute(message, "space", [(t, s) for s, t in ring])
-    whole = call(
+    whole, inverse = call(
         halo_kernel,
-        [(1152, 128)],
-        [i, planes_in, pore, half.reshape(1152, 128)],
+        [(1152, 128), (10, 8, 128)],
+        [i, synthetic_rate, planes_in, pore, half.reshape(1152, 128)],
         1 << 20,
-        ins=[SM, VM, VM, VM],
+        ins=[SM, SM, VM, VM, VM],
     )
     out, moments_new = call(
         final_kernel,

time: 68.2 us -> 68.2 us (level)
  waiting for transfers between devices: 9.92 us -> 7.53 us
  local copies, waits for them, and re-layouts: 0.64 us -> 2.47 us
  Pallas kernels: 9.99 us -> 10.9 us
    ppermute x1, starting transfers between devices: 21.1 us -> 18.3 us  [body(): sums_in = lax.ppermute(packed, ('vel', 'space'), pairs)]
    unnamed x10 -> x12, local copies, waits for them, and re-layouts: 0.64 us -> 2.47 us
    ppermute x1, starting transfers between devices: 3.76 us -> 5.01 us  [body(): right = lax.ppermute(message, 'space', [(t, s) for s, t in ring])]
    all_to_all x1, waiting for transfers between devices: 3.08 us -> 1.88 us  [body(): got = lax.all_to_all(copies, 'vel', 0, 0, axis_index_groups=FAR, tiled=True)]
    ppermute x1, waiting for transfers between devices: 6.83 us -> 5.63 us  [body(): left = lax.ppermute(message, 'space', ring)]
    ppermute x1, starting transfers between devices: 6.32 us -> 7.5 us  [body(): planes_in = lax.ppermute(planes, ('vel', 'space'), pairs)]
    pallas_call x7 -> x8, Pallas kernels: 9.99 us -> 10.9 us  [call(): pl.pallas_call(kernel, out_shape=shapes[0] if single else shapes, in_spec...]
  transfers between devices with their start and end apart: 5 -> 5, of which waited for: 2 -> 2; matrix products, arithmetic and copies ran while one was open for 0% -> 0% of each run, Pallas kernels for 5% -> 2%
where the time goes in v1:
time: 68.2 us; the launch traced here: 67.7 us
  starting transfers between devices  38.6 us (57%)
  Pallas kernels  10.9 us (16%)
  waiting for transfers between devices  7.53 us (11%)
  blocking collectives  7.45 us (11%)
  local copies, waits for them, and re-layouts  2.47 us (4%)
  between operations  0.79 us (1%)
    ppermute x1, starting transfers between devices, body(): sums_in = lax.ppermute(packed, ('vel', 'space'), pairs)  18.3 us
    pallas_call x8, Pallas kernels, call(): pl.pallas_call(kernel, out_shape=shapes[0] if single else shapes, in_spec...  10.9 us
    ppermute x1, starting transfers between devices, body(): planes_in = lax.ppermute(planes, ('vel', 'space'), pairs)  7.5 us
    all_to_all x1, blocking collectives, body(): lax.all_to_all(copies, 'vel', 0, 0, axis_index_groups=NEAR, tiled=True)  7.45 us
    all_to_all x1, starting transfers between devices, body(): got = lax.all_to_all(copies, 'vel', 0, 0, axis_index_groups=FAR, tiled=True)  5.85 us
    ppermute x1, waiting for transfers between devices, body(): left = lax.ppermute(message, 'space', ring)  5.63 us
    ppermute x1, starting transfers between devices, body(): right = lax.ppermute(message, 'space', [(t, s) for s, t in ring])  5.01 us
    unnamed x12, local copies, waits for them, and re-layouts  2.47 us
  transfers between devices with their start and end apart: 5, of which 2 were waited for; matrix products, arithmetic and copies ran while one was open for 0% of the time, Pallas kernels for 2%

profile of v1, /device:TPU:2, one launch (start us, length us, event | category | flops | bytes accessed | tf_op | source)
XLA Modules:
  0.0 67.7 jit_solution(3986835920691105683)
XLA Ops:
  0.6 0.0 copy-start
  0.6 0.0 copy-start.1
  0.7 5.3 %shard_map.60 = (f32[96,128]{1,0:T(8,128)}, f32[144,8,128]{2,1,0:T(8,128)}, f32[7,8,128]{2,1,0:T(8,128)}) custom-call(s32[1]{0:T(128)} %bitcast.i_ref, s32[1]{0:T(128)} %bitcast.10.n_ref, f32[1152,128]{1,0:T(8,128)} %bitcast.33, f32[80,128]{1,0:T(8,128)} %bitcast.36, s32[8,128]{1,0:T(8,128)} %bitcast.42), custom_call_target="tpu_custom_call" | custom-call | flops 1048576 | bytes 4194304 | tf_op jit(solution)/shard_map/pallas_call | solution.py:472
  5.9 0.0 copy-start.3
  5.9 18.3 %collective-permute-start.1 = (f32[96,128]{1,0:T(8,128)}, f32[96,128]{1,0:T(8,128)S(1)}, u32[]{:S(2)}, u32[]{:S(2)}) collective-permute-start(f32[96,128]{1,0:T(8,128)} %get-tuple-element.18), channel_id=1, source_target_pairs={{0,63},{1,0},{2,1},{3,2},{4,3},{5,4},{6,5},{7,6},{8,7},{9,8},{10,9... | collective-permute-start | bytes 147464 | tf_op jit(solution)/shard_map/ppermute | solution.py:537
  24.3 0.0 copy-start.2
  24.3 1.1 %copy-done.2 = f32[144,8,128]{2,1,0:T(8,128)S(1)} copy-done((f32[144,8,128]{2,1,0:T(8,128)S(1)}, f32[144,8,128]{2,1,0:T(8,128)}, u32[]{:S(2)}) %copy-start.2) | copy-done | bytes 589848
  25.4 0.7 %copy-done.4 = f32[7,8,128]{2,1,0:T(8,128)S(1)} copy-done((f32[7,8,128]{2,1,0:T(8,128)S(1)}, f32[7,8,128]{2,1,0:T(8,128)}, u32[]{:S(2)}) %copy-start.4) | copy-done | bytes 28696
  26.1 0.2 shard_map.61
  26.3 0.0 collective-permute-done.1.g_ref
  26.3 0.8 %shard_map.63 = f32[4,80,128]{2,1,0:T(8,128)} custom-call(s32[1]{0:T(128)} %bitcast.i_ref, f32[96,128]{1,0:T(8,128)S(1)} %collective-permute-done.1.g_ref, s32[8,128]{1,0:T(8,128)S(1)} %bitcast.44, f32[7,8,128]{2,1,0:T(8,128)S(1)} %get-tuple-element.19.s_ref), custom_call_target="tpu_custom_call" | custom-call | flops 65536 | bytes 262144 | tf_op jit(solution)/shard_map/pallas_call | solution.py:472
  27.1 5.9 %all-to-all-start = ((f32[4,80,128]{2,1,0:T(8,128)}), f32[4,80,128]{2,1,0:T(8,128)S(1)}, u32[]{:S(2)}, u32[]{:S(2)}) async-start(f32[4,80,128]{2,1,0:T(8,128)} %shard_map.63), calls=%async_computation | async-start | bytes 327680 | tf_op jit(solution)/shard_map/all_to_all | solution.py:556
  33.0 7.5 %collective-permute-start = (f32[600,128]{1,0:T(8,128)S(1)}, f32[600,128]{1,0:T(8,128)S(1)}, u32[]{:S(2)}, u32[]{:S(2)}) collective-permute-start(f32[600,128]{1,0:T(8,128)S(1)} %shard_map.59), channel_id=1, source_target_pairs={{0,63},{1,0},{2,1},{3,2},{4,3},{5,4},{6,5},{7,6},{8,7},{9,8},{10,9... | collective-permute-start | bytes 921608 | tf_op jit(solution)/shard_map/ppermute | solution.py:539
  40.5 1.9 %all-to-all-done.g_ref = f32[4,80,128]{2,1,0:T(8,128)S(1)} async-done(((f32[4,80,128]{2,1,0:T(8,128)}), f32[4,80,128]{2,1,0:T(8,128)S(1)}, u32[]{:S(2)}, u32[]{:S(2)}) %all-to-all-start) | async-done | bytes 163872 | tf_op jit(solution)/shard_map/all_to_all | solution.py:556
  42.4 7.5 %all_to_all.10.g_ref = f32[4,80,128]{2,1,0:T(8,128)S(1)} all-to-all(f32[4,80,128]{2,1,0:T(8,128)S(1)} %shard_map.64), channel_id=1, replica_groups={{0,64,512,576},{128,192,640,704},{256,320,768,832},{384,448,896,960},{1..., dimensions={0} | all-to-all | bytes 327680 | tf_op jit(solution)/shard_map/all_to_all | solution.py:558
  49.9 5.0 %collective-permute-start.3 = (f32[88,128]{1,0:T(8,128)S(1)}, f32[88,128]{1,0:T(8,128)S(1)}, u32[]{:S(2)}, u32[]{:S(2)}) collective-permute-start(f32[88,128]{1,0:T(8,128)S(1)} %get-tuple-element.20), channel_id=1, source_target_pairs={{1,0},{2,1},{3,2},{4,3},{5,4},{6,5},{7,6},{8,7},{9,8},{10,9},{11,1... | collective-permute-start | bytes 135176 | tf_op jit(solution)/shard_map/ppermute | solution.py:564
  54.9 1.9 %collective-permute-start.2 = (f32[88,128]{1,0:T(8,128)S(1)}, f32[88,128]{1,0:T(8,128)S(1)}, u32[]{:S(2)}, u32[]{:S(2)}) collective-permute-start(f32[88,128]{1,0:T(8,128)S(1)} %get-tuple-element.20), channel_id=1, source_target_pairs={{0,1},{1,2},{2,3},{3,4},{4,5},{5,6},{6,7},{7,8},{8,9},{9,10},{10,1... | collective-permute-start | bytes 135176 | tf_op jit(solution)/shard_map/ppermute | solution.py:563
  56.8 0.0 collective-permute-done.g_ref
  56.8 0.0 copy-start.5
  56.8 0.6 copy-done.5
  57.5 1.3 %shard_map.62 = (f32[1152,128]{1,0:T(8,128)S(1)}, f32[10,8,128]{2,1,0:T(8,128)S(1)}) custom-call(s32[1]{0:T(128)} %bitcast.i_ref, f32[10]{0:T(128)S(1)} %copy-done.5, f32[600,128]{1,0:T(8,128)S(1)} %collective-permute-done.g_ref, s32[8,128]{1,0:T(8,128)S(1)} %bitcast.47, f32[1152,128]{1,0:T(8,128)S(1)} %bitcast.40), custom_call_target="tpu_custom_call" | custom-call | flops 1048576 | bytes 4194304 | tf_op jit(solution)/shard_map/pallas_call | solution.py:472
  58.8 0.0 collective-permute-done.3
  58.8 5.6 %collective-permute-done.2 = f32[88,128]{1,0:T(8,128)S(1)} collective-permute-done((f32[88,128]{1,0:T(8,128)S(1)}, f32[88,128]{1,0:T(8,128)S(1)}, u32[]{:S(2)}, u32[]{:S(2)}) %collective-permute-start.2) | collective-permute-done | bytes 45088 | tf_op jit(solution)/shard_map/ppermute | solution.py:563
  64.5 3.3 %shard_map.66 = (f32[144,8,128]{2,1,0:T(8,128)}, f32[10,8,128]{2,1,0:T(8,128)}) custom-call(s32[1]{0:T(128)} %bitcast.i_ref, f32[10,8,128]{2,1,0:T(8,128)S(1)} %get-tuple-element.16.q_ref, f32[144,8,128]{2,1,0:T(8,128)S(1)} %bitcast.41, f32[11,8,128]{2,1,0:T(8,128)S(1)} %bitcast.48, f32[11,8,128]{2,1,0:T(8,128)S(1)} %bitcast.50, f32[11,8,128]{2,1,0:T(8,128)S(1)} %bitcast.49, ...), custom_call_target="tpu_custom_call" | custom-call | flops 1048576 | bytes 4194304 | tf_op jit(solution)/shard_map/pallas_call | solution.py:472
  (7 shorter events, 0.1 us)
Async XLA Ops:
  0.6 23.6 %copy-start = (f32[144,4,256]{2,1,0:T(4,128)S(1)}, f32[144,4,256]{2,1,0:T(4,128)}, u32[]{:S(2)}) copy-start(f32[144,4,256]{2,1,0:T(4,128)} %param.4) | copy-start | bytes 1769476
  0.6 23.6 %copy-start.1 = (f32[10,4,256]{2,1,0:T(4,128)S(1)}, f32[10,4,256]{2,1,0:T(4,128)}, u32[]{:S(2)}) copy-start(f32[10,4,256]{2,1,0:T(4,128)} %param.5) | copy-start | bytes 122884
  5.9 18.4 %copy-start.3 = (s32[4,256]{1,0:T(4,128)S(1)}, s32[4,256]{1,0:T(4,128)}, u32[]{:S(2)}) copy-start(s32[4,256]{1,0:T(4,128)} %param.6) | copy-start | bytes 12292
  5.9 20.4 %collective-permute-start.1 = (f32[96,128]{1,0:T(8,128)}, f32[96,128]{1,0:T(8,128)S(1)}, u32[]{:S(2)}, u32[]{:S(2)}) collective-permute-start(f32[96,128]{1,0:T(8,128)} %get-tuple-element.18), channel_id=1, source_target_pairs={{0,63},{1,0},{2,1},{3,2},{4,3},{5,4},{6,5},{7,6},{8,7},{9,8},{10,9... | collective-permute-start | bytes 147464 | tf_op jit(solution)/shard_map/ppermute | solution.py:537
  24.3 1.1 %copy-start.2 = (f32[144,8,128]{2,1,0:T(8,128)S(1)}, f32[144,8,128]{2,1,0:T(8,128)}, u32[]{:S(2)}) copy-start(f32[144,8,128]{2,1,0:T(8,128)} %get-tuple-element.13.h_hbm) | copy-start | bytes 1769476
  25.4 0.7 %copy-start.4 = (f32[7,8,128]{2,1,0:T(8,128)S(1)}, f32[7,8,128]{2,1,0:T(8,128)}, u32[]{:S(2)}) copy-start(f32[7,8,128]{2,1,0:T(8,128)} %get-tuple-element.14.s_hbm) | copy-start | bytes 86020
  27.1 15.3 %all-to-all-start = ((f32[4,80,128]{2,1,0:T(8,128)}), f32[4,80,128]{2,1,0:T(8,128)S(1)}, u32[]{:S(2)}, u32[]{:S(2)}) async-start(f32[4,80,128]{2,1,0:T(8,128)} %shard_map.63), calls=%async_computation | async-start | bytes 327680 | tf_op jit(solution)/shard_map/all_to_all | solution.py:556
  33.0 23.8 %collective-permute-start = (f32[600,128]{1,0:T(8,128)S(1)}, f32[600,128]{1,0:T(8,128)S(1)}, u32[]{:S(2)}, u32[]{:S(2)}) collective-permute-start(f32[600,128]{1,0:T(8,128)S(1)} %shard_map.59), channel_id=1, source_target_pairs={{0,63},{1,0},{2,1},{3,2},{4,3},{5,4},{6,5},{7,6},{8,7},{9,8},{10,9... | collective-permute-start | bytes 921608 | tf_op jit(solution)/shard_map/ppermute | solution.py:539
  49.9 9.0 %collective-permute-start.3 = (f32[88,128]{1,0:T(8,128)S(1)}, f32[88,128]{1,0:T(8,128)S(1)}, u32[]{:S(2)}, u32[]{:S(2)}) collective-permute-start(f32[88,128]{1,0:T(8,128)S(1)} %get-tuple-element.20), channel_id=1, source_target_pairs={{1,0},{2,1},{3,2},{4,3},{5,4},{6,5},{7,6},{8,7},{9,8},{10,9},{11,1... | collective-permute-start | bytes 135176 | tf_op jit(solution)/shard_map/ppermute | solution.py:564
  54.9 9.6 %collective-permute-start.2 = (f32[88,128]{1,0:T(8,128)S(1)}, f32[88,128]{1,0:T(8,128)S(1)}, u32[]{:S(2)}, u32[]{:S(2)}) collective-permute-start(f32[88,128]{1,0:T(8,128)S(1)} %get-tuple-element.20), channel_id=1, source_target_pairs={{0,1},{1,2},{2,3},{3,4},{4,5},{5,6},{6,7},{7,8},{8,9},{9,10},{10,1... | collective-permute-start | bytes 135176 | tf_op jit(solution)/shard_map/ppermute | solution.py:563
  56.8 0.7 copy-start.5

commit v2 on v1

--- a/solution.py
+++ b/solution.py
@@ -324,16 +324,18 @@
         o_ref[n] = total
 
 
-def change_kernel(g_ref, m_ref, p_ref, o_ref, h_ref):
+def change_kernel(g_ref, m_ref, p_ref, f_ref, o_ref, w_ref, h_ref):
     total = (g_ref[0] + g_ref[1]) + (g_ref[2] + g_ref[3])
+    change = total - m_ref[...]
+    pore = p_ref[...].astype(F)
     h_ref[...] = total
-    o_ref[0:80, :] = total - m_ref[...]
-    o_ref[80:88, :] = p_ref[...].astype(F)
-
-
-def halo_kernel(i_ref, r_ref, g_ref, p_ref, h_ref, o_ref, q_ref):
-    for m in range(10):
-        q_ref[m] = 1.0 / (jnp.full(SHAPE, r_ref[m], F) + 6.0)
+    for ref in (o_ref, w_ref):
+        ref[0:80, :] = change
+        ref[80:88, :] = pore
+    w_ref[88:688, :] = f_ref[...]
+
+
+def halo_kernel(i_ref, u_ref, w_ref, p_ref, h_ref, o_ref):
     a = first_speed(i_ref)
     aa = jnp.abs(a)
     sub, lane = iotas()
@@ -347,8 +349,6 @@
 
     cs = [-2.75 + 0.5 * (4 * t + (sub >> 1)).astype(F) for t in range(3)]
     ecs = [jnp.exp(-c * c) for c in cs]
-    pore_out = pair(g_ref, 596, 597)
-    al = field_polynomial(a, [pair(g_ref, 576 + 2 * m, 577 + 2 * m) for m in range(10)])
     o_ref[...] = h_ref[...]
 
     def back(h, t):
@@ -358,7 +358,9 @@
             return from_z(h, lane, True)
         return jnp.where(sub < 4, from_z(h, lane, False), from_z(h, lane, True))
 
-    def fix(at_0, at_1):
+    def fix(g_ref, start, at_0, at_1):
+        pore_out = pair(g_ref, start + 596, start + 597)
+        al = field_polynomial(a, [pair(g_ref, start + 576 + 2 * m, start + 577 + 2 * m) for m in range(10)])
         pore_0, pore_1 = pair(p_ref, at_0, at_0 + 4), pair(p_ref, at_1, at_1 + 4)
 
         def step(jj, carry):
@@ -375,7 +377,7 @@
                     p0, p1, p2, p3 = polys[side]
                     g = rg * (p0 + c * (p1 + c * (p2 + c * p3)))
                     base = pl.multiple_of(((11 - jj) if side else jj) * 24 + 8 * t, 8)
-                    near, far = g_ref[pl.ds(base, 8), :], g_ref[pl.ds(288 + base, 8), :]
+                    near, far = g_ref[pl.ds(start + base, 8), :], g_ref[pl.ds(start + 288 + base, 8), :]
                     outer = pore_out * (
                         g + wa * far + wb * from_y(near, lane, side == 1, swap_pairs) + wc * back(near, t)
                     )
@@ -392,14 +394,14 @@
 
         lax.fori_loop(0, 6, step, 0)
 
-    pl.when(i_ref[0] >= 8)(lambda: fix(0, 1))
-    pl.when(i_ref[0] < 8)(lambda: fix(3, 2))
+    pl.when(i_ref[0] >= 8)(lambda: fix(u_ref, 0, 0, 1))
+    pl.when(i_ref[0] < 8)(lambda: fix(w_ref, 88, 3, 2))
 
 
 def final_kernel(i_ref, q_ref, h_ref, c_ref, left_ref, right_ref, mh_ref, o_hbm, mo_ref, k_ref, o_ref, sem):
     a = first_speed(i_ref)
     sub, lane = iotas()
-    pores = [left_ref[10], c_ref[10], right_ref[10]]
+    pores = [ref[80:88, :] for ref in (left_ref, c_ref, right_ref)]
     low, high = (sub & 3) == 0, (sub & 3) == 3
     wrap_up, wrap_down = lane < 16, lane >= 112
 
@@ -410,9 +412,9 @@
         return same + swap_halves(other) + from_z(h, lane, True) + from_z(h, lane, False)
 
     for m in range(10):
-        inv = q_ref[m]
+        inv = jnp.broadcast_to(q_ref[m : m + 1, :], SHAPE)
         q = [p * inv for p in pores]
-        change = [left_ref[m], c_ref[m], right_ref[m]]
+        change = [ref[8 * m : 8 * m + 8, :] for ref in (left_ref, c_ref, right_ref)]
         cor = [q[n] * change[n] for n in range(3)]
         for it in range(4):
             new = list(cor)
@@ -501,9 +503,9 @@
 NEAR = groups_of(lambda v: (v % 8) // 2)
 
 
-def upwind_pairs(space):
+def upwind_pairs(space, first=0):
     return [
-        (v * space + s, v * space + (s + (1 if v >= 8 else -1)) % space) for v in range(16) for s in range(space)
+        (v * space + s, v * space + (s + (1 if v >= 8 else -1)) % space) for v in range(first, 16) for s in range(space)
     ]
 
 
@@ -536,7 +538,7 @@
     pairs = upwind_pairs(space)
     sums_in = lax.ppermute(packed, ("vel", "space"), pairs)
     planes = call(planes_kernel, [(600, 128)], [i] + flat, 1 << 16, ins=[SM, VM, VM, VM])
-    planes_in = lax.ppermute(planes, ("vel", "space"), pairs)
+    planes_in = lax.ppermute(planes, ("vel", "space"), upwind_pairs(space, 8))
     half, sums = call(
         late_kernel,
         shapes,
@@ -556,19 +558,24 @@
     got = lax.all_to_all(copies, "vel", 0, 0, axis_index_groups=FAR, tiled=True)
     copies = call(total_kernel, [(4, 80, 128)], [got], 1 << 16, ins=[VM])
     got = lax.all_to_all(copies, "vel", 0, 0, axis_index_groups=NEAR, tiled=True)
-    message, moments_half = call(
-        change_kernel, [(88, 128), (80, 128)], [got, old.reshape(80, 128), pore], 1 << 16, ins=[VM] * 3
+    message, message_down, moments_half = call(
+        change_kernel,
+        [(88, 128), (688, 128), (80, 128)],
+        [got, old.reshape(80, 128), pore, planes],
+        1 << 16,
+        ins=[VM] * 4,
     )
     ring = [(s, (s + 1) % space) for s in range(space)]
     left = lax.ppermute(message, "space", ring)
-    right = lax.ppermute(message, "space", [(t, s) for s, t in ring])
-    whole, inverse = call(
+    right = lax.ppermute(message_down, "space", [(t, s) for s, t in ring])
+    whole = call(
         halo_kernel,
-        [(1152, 128), (10, 8, 128)],
-        [i, synthetic_rate, planes_in, pore, half.reshape(1152, 128)],
+        [(1152, 128)],
+        [i, planes_in, right, pore, half.reshape(1152, 128)],
         1 << 20,
-        ins=[SM, SM, VM, VM, VM],
-    )
+        ins=[SM, VM, VM, VM, VM],
+    )
+    inverse = jnp.broadcast_to((1.0 / (synthetic_rate + 6.0))[:, None], (10, 128))
     out, moments_new = call(
         final_kernel,
         [(144, 8, 128), (10, 8, 128)],
@@ -576,9 +583,9 @@
             i,
             inverse,
             whole.reshape(144, 8, 128),
-            message.reshape(11, 8, 128),
-            left.reshape(11, 8, 128),
-            right.reshape(11, 8, 128),
+            message,
+            left,
+            right,
             moments_half.reshape(10, 8, 128),
         ],
         1 << 20,

time: 68.2 us -> 72.7 us (1.066)
  the two profiles are of different devices: /device:TPU:2 before, /device:TPU:16 now
where the time goes in v2:
time: 72.7 us; the launch traced here: 72.2 us
  waiting for transfers between devices  28.1 us (39%)
  blocking collectives  16 us (22%)
  starting transfers between devices  15 us (21%)
  Pallas kernels  10.4 us (14%)
  local copies, waits for them, and re-layouts  1.9 us (3%)
  between operations  0.8 us (1%)
    all_to_all x1, blocking collectives, body(): got = lax.all_to_all(copies, 'vel', 0, 0, axis_index_groups=FAR, tiled=True)  16 us
    ppermute x1, waiting for transfers between devices, body(): sums_in = lax.ppermute(packed, ('vel', 'space'), pairs)  15.4 us
    pallas_call x8, Pallas kernels, call(): pl.pallas_call(kernel, out_shape=shapes[0] if single else shapes, in_spec...  10.4 us
    ppermute x1, waiting for transfers between devices, body(): planes_in = lax.ppermute(planes, ('vel', 'space'), upwind_pairs(space, 8))  8.61 us
    ppermute x1, starting transfers between devices, body(): right = lax.ppermute(message_down, 'space', [(t, s) for s, t in ring])  5.13 us
    all_to_all x1, starting transfers between devices, body(): lax.all_to_all(copies, 'vel', 0, 0, axis_index_groups=NEAR, tiled=True)  4.15 us
    all_to_all x1, waiting for transfers between devices, body(): lax.all_to_all(copies, 'vel', 0, 0, axis_index_groups=NEAR, tiled=True)  4.06 us
    ppermute x1, starting transfers between devices, body(): planes_in = lax.ppermute(planes, ('vel', 'space'), upwind_pairs(space, 8))  1.92 us
  transfers between devices with their start and end apart: 5, of which 3 were waited for; matrix products, arithmetic and copies ran while one was open for 0% of the time, Pallas kernels for 1%

profile of v2, /device:TPU:16, one launch (start us, length us, event | category | flops | bytes accessed | tf_op | source)
XLA Modules:
  0.0 72.2 jit_solution(14223282794302268906)
XLA Ops:
  0.6 0.0 copy-start.1
  0.7 5.3 %shard_map.60 = (f32[96,128]{1,0:T(8,128)}, f32[144,8,128]{2,1,0:T(8,128)}, f32[7,8,128]{2,1,0:T(8,128)}) custom-call(s32[1]{0:T(128)} %bitcast.i_ref, s32[1]{0:T(128)} %bitcast.10.n_ref, f32[1152,128]{1,0:T(8,128)} %bitcast.30, f32[80,128]{1,0:T(8,128)} %bitcast.34, s32[8,128]{1,0:T(8,128)} %bitcast.39), custom_call_target="tpu_custom_call" | custom-call | flops 1048576 | bytes 4194304 | tf_op jit(solution)/shard_map/pallas_call | solution.py:474
  5.9 0.0 copy-start.3
  6.0 1.9 %collective-permute-start.1 = (f32[96,128]{1,0:T(8,128)}, f32[96,128]{1,0:T(8,128)S(1)}, u32[]{:S(2)}, u32[]{:S(2)}) collective-permute-start(f32[96,128]{1,0:T(8,128)} %get-tuple-element.12), channel_id=1, source_target_pairs={{0,63},{1,0},{2,1},{3,2},{4,3},{5,4},{6,5},{7,6},{8,7},{9,8},{10,9... | collective-permute-start | bytes 147464 | tf_op jit(solution)/shard_map/ppermute | solution.py:539
  7.9 0.0 copy-start.2
  7.9 1.1 %copy-done.2 = f32[144,8,128]{2,1,0:T(8,128)S(1)} copy-done((f32[144,8,128]{2,1,0:T(8,128)S(1)}, f32[144,8,128]{2,1,0:T(8,128)}, u32[]{:S(2)}) %copy-start.2) | copy-done | bytes 589848
  9.0 0.7 %copy-done.4 = f32[7,8,128]{2,1,0:T(8,128)S(1)} copy-done((f32[7,8,128]{2,1,0:T(8,128)S(1)}, f32[7,8,128]{2,1,0:T(8,128)}, u32[]{:S(2)}) %copy-start.4) | copy-done | bytes 28696
  9.7 0.2 shard_map.61
  9.9 15.4 %collective-permute-done.1.g_ref = f32[96,128]{1,0:T(8,128)S(1)} collective-permute-done((f32[96,128]{1,0:T(8,128)}, f32[96,128]{1,0:T(8,128)S(1)}, u32[]{:S(2)}, u32[]{:S(2)}) %collective-permute-start.1) | collective-permute-done | bytes 49184 | tf_op jit(solution)/shard_map/ppermute | solution.py:539
  25.4 0.1 shard_map.62
  25.5 16.0 %all_to_all.10.g_ref = f32[4,80,128]{2,1,0:T(8,128)S(1)} all-to-all(f32[4,80,128]{2,1,0:T(8,128)S(1)} %shard_map.62), channel_id=1, replica_groups={{0,128,256,384},{64,192,320,448},{512,640,768,896},{576,704,832,960},{1..., dimensions={0} | all-to-all | bytes 327680 | tf_op jit(solution)/shard_map/all_to_all | solution.py:558
  41.5 0.7 shard_map.63
  42.1 4.2 %all-to-all-start.1 = ((f32[4,80,128]{2,1,0:T(8,128)}), f32[4,80,128]{2,1,0:T(8,128)S(1)}, u32[]{:S(2)}, u32[]{:S(2)}) async-start(f32[4,80,128]{2,1,0:T(8,128)} %shard_map.63), calls=%async_computation.1 | async-start | bytes 327680 | tf_op jit(solution)/shard_map/all_to_all | solution.py:560
  46.3 4.1 %all-to-all-done.1.g_ref = f32[4,80,128]{2,1,0:T(8,128)S(1)} async-done(((f32[4,80,128]{2,1,0:T(8,128)}), f32[4,80,128]{2,1,0:T(8,128)S(1)}, u32[]{:S(2)}, u32[]{:S(2)}) %all-to-all-start.1) | async-done | bytes 163872 | tf_op jit(solution)/shard_map/all_to_all | solution.py:560
  50.4 0.0 copy-start.5
  50.4 5.1 %collective-permute-start.2 = (f32[688,128]{1,0:T(8,128)S(1)}, f32[688,128]{1,0:T(8,128)S(1)}, u32[]{:S(2)}, u32[]{:S(2)}) collective-permute-start(f32[688,128]{1,0:T(8,128)S(1)} %get-tuple-element.16), channel_id=1, source_target_pairs={{1,0},{2,1},{3,2},{4,3},{5,4},{6,5},{7,6},{8,7},{9,8},{10,9},{11,1... | collective-permute-start | bytes 1056776 | tf_op jit(solution)/shard_map/ppermute | solution.py:570
  55.6 1.9 %collective-permute-start = (f32[600,128]{1,0:T(8,128)S(1)}, f32[600,128]{1,0:T(8,128)S(1)}, u32[]{:S(2)}, u32[]{:S(2)}) collective-permute-start(f32[600,128]{1,0:T(8,128)S(1)} %shard_map.59.f_ref), channel_id=1, source_target_pairs={{512,513},{513,514},{514,515},{515,516},{516,517},{517,518},{518,5... | collective-permute-start | bytes 921608 | tf_op jit(solution)/shard_map/ppermute | solution.py:541
  57.5 1.9 %collective-permute-start.3 = (f32[88,128]{1,0:T(8,128)S(1)}, f32[88,128]{1,0:T(8,128)S(1)}, u32[]{:S(2)}, u32[]{:S(2)}) collective-permute-start(f32[88,128]{1,0:T(8,128)S(1)} %get-tuple-element.18.c_ref), channel_id=1, source_target_pairs={{0,1},{1,2},{2,3},{3,4},{4,5},{5,6},{6,7},{7,8},{8,9},{9,10},{10,1... | collective-permute-start | bytes 135176 | tf_op jit(solution)/shard_map/ppermute | solution.py:569
  59.5 8.6 %collective-permute-done.u_ref = f32[600,128]{1,0:T(8,128)S(1)} collective-permute-done((f32[600,128]{1,0:T(8,128)S(1)}, f32[600,128]{1,0:T(8,128)S(1)}, u32[]{:S(2)}, u32[]{:S(2)}) %collective-permute-start) | collective-permute-done | bytes 307232 | tf_op jit(solution)/shard_map/ppermute | solution.py:541
  68.1 0.0 collective-permute-done.2.w_ref.right_ref
  68.1 0.8 %shard_map.65 = f32[1152,128]{1,0:T(8,128)S(1)} custom-call(s32[1]{0:T(128)} %bitcast.i_ref, f32[600,128]{1,0:T(8,128)S(1)} %collective-permute-done.u_ref, f32[688,128]{1,0:T(8,128)S(1)} %collective-permute-done.2.w_ref.right_ref, s32[8,128]{1,0:T(8,128)S(1)} %bitcast.44, f32[1152,128]{1,0:T(8,128)S(1)} %bitcast.38), custom_call_target="tpu_custom_call" | custom-call | flops 1048576 | bytes 4194304 | tf_op jit(solution)/shard_map/pallas_call | solution.py:474
  68.9 0.0 collective-permute-done.3.left_ref
  68.9 0.1 broadcast_in_dim.2.q_ref
  69.0 3.3 %shard_map.66 = (f32[144,8,128]{2,1,0:T(8,128)}, f32[10,8,128]{2,1,0:T(8,128)}) custom-call(s32[1]{0:T(128)} %bitcast.i_ref, f32[10,128]{1,0:T(8,128)S(1)} %broadcast_in_dim.2.q_ref, f32[144,8,128]{2,1,0:T(8,128)S(1)} %bitcast.33, f32[88,128]{1,0:T(8,128)S(1)} %get-tuple-element.18.c_ref, f32[88,128]{1,0:T(8,128)S(1)} %collective-permute-done.3.left_ref, ...), custom_call_target="tpu_custom_call" | custom-call | flops 1048576 | bytes 4194304 | tf_op jit(solution)/shard_map/pallas_call | solution.py:474
  (9 shorter events, 0.1 us)
Async XLA Ops:
  0.6 7.3 %copy-start = (f32[144,4,256]{2,1,0:T(4,128)S(1)}, f32[144,4,256]{2,1,0:T(4,128)}, u32[]{:S(2)}) copy-start(f32[144,4,256]{2,1,0:T(4,128)} %param.4) | copy-start | bytes 1769476
  0.6 7.2 %copy-start.1 = (f32[10,4,256]{2,1,0:T(4,128)S(1)}, f32[10,4,256]{2,1,0:T(4,128)}, u32[]{:S(2)}) copy-start(f32[10,4,256]{2,1,0:T(4,128)} %param.5) | copy-start | bytes 122884
  5.9 2.0 %copy-start.3 = (s32[4,256]{1,0:T(4,128)S(1)}, s32[4,256]{1,0:T(4,128)}, u32[]{:S(2)}) copy-start(s32[4,256]{1,0:T(4,128)} %param.6) | copy-start | bytes 12292
  6.0 19.4 %collective-permute-start.1 = (f32[96,128]{1,0:T(8,128)}, f32[96,128]{1,0:T(8,128)S(1)}, u32[]{:S(2)}, u32[]{:S(2)}) collective-permute-start(f32[96,128]{1,0:T(8,128)} %get-tuple-element.12), channel_id=1, source_target_pairs={{0,63},{1,0},{2,1},{3,2},{4,3},{5,4},{6,5},{7,6},{8,7},{9,8},{10,9... | collective-permute-start | bytes 147464 | tf_op jit(solution)/shard_map/ppermute | solution.py:539
  7.9 1.1 %copy-start.2 = (f32[144,8,128]{2,1,0:T(8,128)S(1)}, f32[144,8,128]{2,1,0:T(8,128)}, u32[]{:S(2)}) copy-start(f32[144,8,128]{2,1,0:T(8,128)} %get-tuple-element.13.h_hbm) | copy-start | bytes 1769476
  9.0 0.7 %copy-start.4 = (f32[7,8,128]{2,1,0:T(8,128)S(1)}, f32[7,8,128]{2,1,0:T(8,128)}, u32[]{:S(2)}) copy-start(f32[7,8,128]{2,1,0:T(8,128)} %get-tuple-element.14.s_hbm) | copy-start | bytes 86020
  42.1 8.2 %all-to-all-start.1 = ((f32[4,80,128]{2,1,0:T(8,128)}), f32[4,80,128]{2,1,0:T(8,128)S(1)}, u32[]{:S(2)}, u32[]{:S(2)}) async-start(f32[4,80,128]{2,1,0:T(8,128)} %shard_map.63), calls=%async_computation.1 | async-start | bytes 327680 | tf_op jit(solution)/shard_map/all_to_all | solution.py:560
  50.4 9.0 %copy-start.5 = (f32[10]{0:T(128)S(1)}, f32[10]{0:T(128)}, u32[]{:S(2)}) copy-start(f32[10]{0:T(128)} %param.7) | copy-start | bytes 124
  50.4 17.6 %collective-permute-start.2 = (f32[688,128]{1,0:T(8,128)S(1)}, f32[688,128]{1,0:T(8,128)S(1)}, u32[]{:S(2)}, u32[]{:S(2)}) collective-permute-start(f32[688,128]{1,0:T(8,128)S(1)} %get-tuple-element.16), channel_id=1, source_target_pairs={{1,0},{2,1},{3,2},{4,3},{5,4},{6,5},{7,6},{8,7},{9,8},{10,9},{11,1... | collective-permute-start | bytes 1056776 | tf_op jit(solution)/shard_map/ppermute | solution.py:570
  55.6 12.5 %collective-permute-start = (f32[600,128]{1,0:T(8,128)S(1)}, f32[600,128]{1,0:T(8,128)S(1)}, u32[]{:S(2)}, u32[]{:S(2)}) collective-permute-start(f32[600,128]{1,0:T(8,128)S(1)} %shard_map.59.f_ref), channel_id=1, source_target_pairs={{512,513},{513,514},{514,515},{515,516},{516,517},{517,518},{518,5... | collective-permute-start | bytes 921608 | tf_op jit(solution)/shard_map/ppermute | solution.py:541
  57.5 11.4 %collective-permute-start.3 = (f32[88,128]{1,0:T(8,128)S(1)}, f32[88,128]{1,0:T(8,128)S(1)}, u32[]{:S(2)}, u32[]{:S(2)}) collective-permute-start(f32[88,128]{1,0:T(8,128)S(1)} %get-tuple-element.18.c_ref), channel_id=1, source_target_pairs={{0,1},{1,2},{2,3},{3,4},{4,5},{5,6},{6,7},{7,8},{8,9},{9,10},{10,1... | collective-permute-start | bytes 135176 | tf_op jit(solution)/shard_map/ppermute | solution.py:569

commit v3 on v1

--- a/solution.py
+++ b/solution.py
@@ -1,3 +1,4 @@
+import functools
 import math
 
 import jax
@@ -87,12 +88,18 @@
 
 
 def sums_kernel(i_ref, n_ref, x_hbm, m_hbm, p_hbm, g_ref, h_hbm, s_hbm, x_ref, m_ref, p_ref, h_ref, s_ref, sem):
+    def rows_of(j):
+        rows = pl.ds(96 * j, 96)
+        return pltpu.make_async_copy(x_hbm.at[rows], x_ref.at[rows], sem.at[2 + j])
+
     copies = [
-        pltpu.make_async_copy(src, dst, sem.at[n])
-        for n, (src, dst) in enumerate(((x_hbm, x_ref), (m_hbm, m_ref), (p_hbm, p_ref)))
+        pltpu.make_async_copy(src, dst, sem.at[n]) for n, (src, dst) in enumerate(((m_hbm, m_ref), (p_hbm, p_ref)))
     ]
     for copy in copies:
         copy.start()
+    for j in range(6):
+        rows_of(j).start()
+        rows_of(11 - j).start()
     a = first_speed(i_ref)
     aa = jnp.abs(a)
     sub, lane = iotas()
@@ -123,6 +130,8 @@
 
         def step(jj, carry):
             whole, down, up, minus, plus, double = carry
+            rows_of(jj).wait()
+            rows_of(11 - jj).wait()
             bm = 2.75 - 0.5 * jj.astype(F)
             ex = jnp.exp(-(a * a) - bm * bm)
             polys = [at_second(al, -bm), at_second(al, bm)]
@@ -331,9 +340,11 @@
     o_ref[80:88, :] = p_ref[...].astype(F)
 
 
-def halo_kernel(i_ref, r_ref, g_ref, p_ref, h_ref, o_ref, q_ref):
-    for m in range(10):
-        q_ref[m] = 1.0 / (jnp.full(SHAPE, r_ref[m], F) + 6.0)
+def halo_kernel(wanted, i_ref, n_ref, *refs):
+    pl.when(early(n_ref) if wanted else jnp.logical_not(early(n_ref)))(lambda: add_halo(i_ref, *refs))
+
+
+def add_halo(i_ref, g_ref, p_ref, h_ref, o_ref):
     a = first_speed(i_ref)
     aa = jnp.abs(a)
     sub, lane = iotas()
@@ -396,21 +407,24 @@
     pl.when(i_ref[0] < 8)(lambda: fix(3, 2))
 
 
-def final_kernel(i_ref, q_ref, h_ref, c_ref, left_ref, right_ref, mh_ref, o_hbm, mo_ref, k_ref, o_ref, sem):
+def final_kernel(i_ref, n_ref, q_ref, e_ref, l_ref, c_ref, left_ref, right_ref, mh_ref, o_hbm, mo_ref, k_ref, o_ref, sem):
     a = first_speed(i_ref)
     sub, lane = iotas()
     pores = [left_ref[10], c_ref[10], right_ref[10]]
     low, high = (sub & 3) == 0, (sub & 3) == 3
     wrap_up, wrap_down = lane < 16, lane >= 112
+    z_first, z_last = (lane & 15) == 0, (lane & 15) == 15
 
     def around(h):
         up, down = pltpu.roll(h, 16, 1), pltpu.roll(h, 112, 1)
         same = jnp.where(wrap_up, 0.0, up) + jnp.where(wrap_down, 0.0, down)
         other = jnp.where(wrap_up, up, jnp.where(wrap_down, down, 0.0))
-        return same + swap_halves(other) + from_z(h, lane, True) + from_z(h, lane, False)
+        forth = pltpu.roll(jnp.where(z_last, down, h), 1, 1)
+        back = pltpu.roll(jnp.where(z_first, up, h), 127, 1)
+        return same + swap_halves(other) + (forth + back)
 
     for m in range(10):
-        inv = q_ref[m]
+        inv = jnp.broadcast_to(q_ref[m : m + 1, :], SHAPE)
         q = [p * inv for p in pores]
         change = [left_ref[m], c_ref[m], right_ref[m]]
         cor = [q[n] * change[n] for n in range(3)]
@@ -437,7 +451,10 @@
         rows = pl.ds(j * 12, 12)
         return pltpu.make_async_copy(o_ref.at[rows], o_hbm.at[rows], sem.at[n])
 
-    def step(jj, carry):
+    def lift(h_ref):
+        lax.fori_loop(0, 6, functools.partial(step, h_ref), 0)
+
+    def step(h_ref, jj, carry):
         bm = 2.75 - 0.5 * jj.astype(F)
         ex = pore * jnp.exp(-(a * a) - bm * bm)
         for side in range(2):
@@ -454,7 +471,8 @@
             chunk(6 * side + jj, j).start()
         return carry
 
-    lax.fori_loop(0, 6, step, 0)
+    pl.when(early(n_ref))(lambda: lift(e_ref))
+    pl.when(jnp.logical_not(early(n_ref)))(lambda: lift(l_ref))
     for jj in range(6):
         chunk(jj, jj).wait()
         chunk(6 + jj, 11 - jj).wait()
@@ -527,7 +545,7 @@
             pltpu.VMEM((8, 128), jnp.int32),
             pltpu.VMEM((144, 8, 128), F),
             pltpu.VMEM((7, 8, 128), F),
-            pltpu.SemaphoreType.DMA((3,)),
+            pltpu.SemaphoreType.DMA((14,)),
         ],
         [SM, SM, HBM, HBM, HBM],
         [VM, HBM, HBM],
@@ -560,22 +578,22 @@
         change_kernel, [(88, 128), (80, 128)], [got, old.reshape(80, 128), pore], 1 << 16, ins=[VM] * 3
     )
     ring = [(s, (s + 1) % space) for s in range(space)]
+    args = [i, n, planes_in, pore, half.reshape(1152, 128)]
+    ins = [SM, SM, VM, VM, VM]
     left = lax.ppermute(message, "space", ring)
+    whole_early = call(functools.partial(halo_kernel, True), [(1152, 128)], args, 1 << 16, ins=ins)
     right = lax.ppermute(message, "space", [(t, s) for s, t in ring])
-    whole, inverse = call(
-        halo_kernel,
-        [(1152, 128), (10, 8, 128)],
-        [i, synthetic_rate, planes_in, pore, half.reshape(1152, 128)],
-        1 << 20,
-        ins=[SM, SM, VM, VM, VM],
-    )
+    whole_late = call(functools.partial(halo_kernel, False), [(1152, 128)], args, 1 << 20, ins=ins)
+    inverse = jnp.broadcast_to((1.0 / (synthetic_rate + 6.0))[:, None], (10, 128))
     out, moments_new = call(
         final_kernel,
         [(144, 8, 128), (10, 8, 128)],
         [
             i,
+            n,
             inverse,
-            whole.reshape(144, 8, 128),
+            whole_early.reshape(144, 8, 128),
+            whole_late.reshape(144, 8, 128),
             message.reshape(11, 8, 128),
             left.reshape(11, 8, 128),
             right.reshape(11, 8, 128),
@@ -583,7 +601,7 @@
         ],
         1 << 20,
         [pltpu.VMEM((10, 8, 128), F), pltpu.VMEM((144, 8, 128), F), pltpu.SemaphoreType.DMA((12,))],
-        [SM] + [VM] * 6,
+        [SM, SM] + [VM] * 7,
         [HBM, VM],
     )
     return from_registers(out), from_registers(moments_new)

time: 68.2 us -> 66.8 us (0.979)
  blocking collectives: 7.45 us -> 15.3 us
  waiting for transfers between devices: 7.53 us -> 0.84 us
  Pallas kernels: 10.9 us -> 9.27 us
    all_to_all x1, blocking collectives: 7.45 us -> 15.3 us  [body(): got = lax.all_to_all(copies, 'vel', 0, 0, axis_index_groups=FAR, tiled=True)]
    ppermute x1, waiting for transfers between devices: 5.63 us -> 0.01 us  [body(): left = lax.ppermute(message, 'space', ring)]
    ppermute x1, starting transfers between devices: 5.01 us -> 7.86 us  [body(): right = lax.ppermute(message, 'space', [(t, s) for s, t in ring])]
    all_to_all x1, waiting for transfers between devices: 1.88 us -> 0.01 us  [body(): lax.all_to_all(copies, 'vel', 0, 0, axis_index_groups=NEAR, tiled=True)]
    all_to_all x1, starting transfers between devices: 5.85 us -> 4.06 us  [body(): lax.all_to_all(copies, 'vel', 0, 0, axis_index_groups=NEAR, tiled=True)]
    pallas_call x8 -> x9, Pallas kernels: 10.9 us -> 9.27 us  [call(): pl.pallas_call(kernel, out_shape=shapes[0] if single else shapes, in_spec...]
    ppermute x1, starting transfers between devices: 7.5 us -> 6 us  [body(): planes_in = lax.ppermute(planes, ('vel', 'space'), pairs)]
    ppermute x1, waiting for transfers between devices: 0.01 us -> 0.82 us  [body(): right = lax.ppermute(message, 'space', [(t, s) for s, t in ring])]
  transfers between devices with their start and end apart: 5 -> 5, of which waited for: 2 -> 1; matrix products, arithmetic and copies ran while one was open for 0% -> 0% of each run, Pallas kernels for 2% -> 2%
where the time goes in v3:
time: 66.8 us; the launch traced here: 66.3 us
  starting transfers between devices  38.2 us (57%)
  blocking collectives  15.3 us (23%)
  Pallas kernels  9.27 us (14%)
  local copies, waits for them, and re-layouts  1.9 us (3%)
  waiting for transfers between devices  0.84 us (1%)
  between operations  0.82 us (1%)
    ppermute x1, starting transfers between devices, body(): sums_in = lax.ppermute(packed, ('vel', 'space'), pairs)  18.3 us
    all_to_all x1, blocking collectives, body(): got = lax.all_to_all(copies, 'vel', 0, 0, axis_index_groups=FAR, tiled=True)  15.3 us
    pallas_call x9, Pallas kernels, call(): pl.pallas_call(kernel, out_shape=shapes[0] if single else shapes, in_spec...  9.27 us
    ppermute x1, starting transfers between devices, body(): right = lax.ppermute(message, 'space', [(t, s) for s, t in ring])  7.86 us
    ppermute x1, starting transfers between devices, body(): planes_in = lax.ppermute(planes, ('vel', 'space'), pairs)  6 us
    all_to_all x1, starting transfers between devices, body(): lax.all_to_all(copies, 'vel', 0, 0, axis_index_groups=NEAR, tiled=True)  4.06 us
    ppermute x1, starting transfers between devices, body(): left = lax.ppermute(message, 'space', ring)  1.92 us
    unnamed x12, local copies, waits for them, and re-layouts  1.83 us
  transfers between devices with their start and end apart: 5, of which 1 were waited for; matrix products, arithmetic and copies ran while one was open for 0% of the time, Pallas kernels for 2%

profile of v3, /device:TPU:2, one launch (start us, length us, event | category | flops | bytes accessed | tf_op | source)
XLA Modules:
  0.0 66.3 jit_solution(168487585093317176)
XLA Ops:
  0.7 5.1 %shard_map.60 = (f32[96,128]{1,0:T(8,128)}, f32[144,8,128]{2,1,0:T(8,128)}, f32[7,8,128]{2,1,0:T(8,128)}) custom-call(s32[1]{0:T(128)} %bitcast.i_ref, s32[1]{0:T(128)} %bitcast.1.n_ref, f32[1152,128]{1,0:T(8,128)} %bitcast.34, f32[80,128]{1,0:T(8,128)} %bitcast.41, s32[8,128]{1,0:T(8,128)} %bitcast.45), custom_call_target="tpu_custom_call" | custom-call | flops 1048576 | bytes 4194304 | tf_op jit(solution)/shard_map/pallas_call | solution.py:490
  5.8 0.0 copy-start.3
  5.8 18.3 %collective-permute-start.1 = (f32[96,128]{1,0:T(8,128)}, f32[96,128]{1,0:T(8,128)S(1)}, u32[]{:S(2)}, u32[]{:S(2)}) collective-permute-start(f32[96,128]{1,0:T(8,128)} %get-tuple-element.14), channel_id=1, source_target_pairs={{0,63},{1,0},{2,1},{3,2},{4,3},{5,4},{6,5},{7,6},{8,7},{9,8},{10,9... | collective-permute-start | bytes 147464 | tf_op jit(solution)/shard_map/ppermute | solution.py:555
  24.2 0.0 copy-start.2
  24.2 1.1 %copy-done.2 = f32[144,8,128]{2,1,0:T(8,128)S(1)} copy-done((f32[144,8,128]{2,1,0:T(8,128)S(1)}, f32[144,8,128]{2,1,0:T(8,128)}, u32[]{:S(2)}) %copy-start.2) | copy-done | bytes 589848
  25.3 0.7 %copy-done.4 = f32[7,8,128]{2,1,0:T(8,128)S(1)} copy-done((f32[7,8,128]{2,1,0:T(8,128)S(1)}, f32[7,8,128]{2,1,0:T(8,128)}, u32[]{:S(2)}) %copy-start.4) | copy-done | bytes 28696
  26.0 0.2 shard_map.61
  26.2 0.0 collective-permute-done.1.g_ref
  26.2 0.1 shard_map.64
  26.3 15.3 %all_to_all.10.g_ref = f32[4,80,128]{2,1,0:T(8,128)S(1)} all-to-all(f32[4,80,128]{2,1,0:T(8,128)S(1)} %shard_map.64), channel_id=1, replica_groups={{0,128,256,384},{64,192,320,448},{512,640,768,896},{576,704,832,960},{1..., dimensions={0} | all-to-all | bytes 327680 | tf_op jit(solution)/shard_map/all_to_all | solution.py:574
  41.6 0.7 %shard_map.65 = f32[4,80,128]{2,1,0:T(8,128)} custom-call(f32[4,80,128]{2,1,0:T(8,128)S(1)} %all_to_all.10.g_ref), custom_call_target="tpu_custom_call" | custom-call | flops 65536 | bytes 262144 | tf_op jit(solution)/shard_map/pallas_call | solution.py:490
  42.3 4.1 %all-to-all-start.1 = ((f32[4,80,128]{2,1,0:T(8,128)}), f32[4,80,128]{2,1,0:T(8,128)S(1)}, u32[]{:S(2)}, u32[]{:S(2)}) async-start(f32[4,80,128]{2,1,0:T(8,128)} %shard_map.65), calls=%async_computation.1 | async-start | bytes 327680 | tf_op jit(solution)/shard_map/all_to_all | solution.py:576
  46.4 6.0 %collective-permute-start = (f32[600,128]{1,0:T(8,128)S(1)}, f32[600,128]{1,0:T(8,128)S(1)}, u32[]{:S(2)}, u32[]{:S(2)}) collective-permute-start(f32[600,128]{1,0:T(8,128)S(1)} %shard_map.59), channel_id=1, source_target_pairs={{0,63},{1,0},{2,1},{3,2},{4,3},{5,4},{6,5},{7,6},{8,7},{9,8},{10,9... | collective-permute-start | bytes 921608 | tf_op jit(solution)/shard_map/ppermute | solution.py:557
  52.4 0.0 all-to-all-done.1.g_ref
  52.4 0.0 copy-start.5
  52.5 1.9 %collective-permute-start.2 = (f32[88,128]{1,0:T(8,128)S(1)}, f32[88,128]{1,0:T(8,128)S(1)}, u32[]{:S(2)}, u32[]{:S(2)}) collective-permute-start(f32[88,128]{1,0:T(8,128)S(1)} %get-tuple-element.16), channel_id=1, source_target_pairs={{0,1},{1,2},{2,3},{3,4},{4,5},{5,6},{6,7},{7,8},{8,9},{9,10},{10,1... | collective-permute-start | bytes 135176 | tf_op jit(solution)/shard_map/ppermute | solution.py:583
  54.4 7.9 %collective-permute-start.3 = (f32[88,128]{1,0:T(8,128)S(1)}, f32[88,128]{1,0:T(8,128)S(1)}, u32[]{:S(2)}, u32[]{:S(2)}) collective-permute-start(f32[88,128]{1,0:T(8,128)S(1)} %get-tuple-element.16), channel_id=1, source_target_pairs={{1,0},{2,1},{3,2},{4,3},{5,4},{6,5},{7,6},{8,7},{9,8},{10,9},{11,1... | collective-permute-start | bytes 135176 | tf_op jit(solution)/shard_map/ppermute | solution.py:585
  62.3 0.0 copy-done.5
  62.3 0.0 collective-permute-done.refs_0_
  62.3 0.8 %shard_map.62 = f32[1152,128]{1,0:T(8,128)S(1)} custom-call(s32[1]{0:T(128)} %bitcast.i_ref, s32[1]{0:T(128)} %bitcast.1.n_ref, f32[600,128]{1,0:T(8,128)S(1)} %collective-permute-done.refs_0_, s32[8,128]{1,0:T(8,128)S(1)} %bitcast.50, f32[1152,128]{1,0:T(8,128)S(1)} %bitcast.37), custom_call_target="tpu_custom_call" | custom-call | flops 65536 | bytes 262144 | tf_op jit(solution)/shard_map/pallas_call | solution.py:490
  63.1 0.0 collective-permute-done.2
  63.1 0.8 %collective-permute-done.3 = f32[88,128]{1,0:T(8,128)S(1)} collective-permute-done((f32[88,128]{1,0:T(8,128)S(1)}, f32[88,128]{1,0:T(8,128)S(1)}, u32[]{:S(2)}, u32[]{:S(2)}) %collective-permute-start.3) | collective-permute-done | bytes 45088 | tf_op jit(solution)/shard_map/ppermute | solution.py:585
  64.0 0.1 broadcast_in_dim.2.q_ref
  64.0 2.3 %shard_map.67 = (f32[144,8,128]{2,1,0:T(8,128)}, f32[10,8,128]{2,1,0:T(8,128)}) custom-call(s32[1]{0:T(128)} %bitcast.i_ref, s32[1]{0:T(128)} %bitcast.1.n_ref, f32[10,128]{1,0:T(8,128)S(1)} %broadcast_in_dim.2.q_ref, f32[144,8,128]{2,1,0:T(8,128)S(1)} %bitcast.39, f32[144,8,128]{2,1,0:T(8,128)S(1)} %bitcast.40, f32[11,8,128]{2,1,0:T(8,128)S(1)} %bitcast.52, ...), custom_call_target="tpu_custom_call" | custom-call | flops 1048576 | bytes 4194304 | tf_op jit(solution)/shard_map/pallas_call | solution.py:490
  (10 shorter events, 0.1 us)
Async XLA Ops:
  0.6 23.5 %copy-start = (f32[144,4,256]{2,1,0:T(4,128)S(1)}, f32[144,4,256]{2,1,0:T(4,128)}, u32[]{:S(2)}) copy-start(f32[144,4,256]{2,1,0:T(4,128)} %param.4) | copy-start | bytes 1769476
  0.6 23.5 %copy-start.1 = (f32[10,4,256]{2,1,0:T(4,128)S(1)}, f32[10,4,256]{2,1,0:T(4,128)}, u32[]{:S(2)}) copy-start(f32[10,4,256]{2,1,0:T(4,128)} %param.5) | copy-start | bytes 122884
  5.8 18.4 %copy-start.3 = (s32[4,256]{1,0:T(4,128)S(1)}, s32[4,256]{1,0:T(4,128)}, u32[]{:S(2)}) copy-start(s32[4,256]{1,0:T(4,128)} %param.6) | copy-start | bytes 12292
  5.8 20.4 %collective-permute-start.1 = (f32[96,128]{1,0:T(8,128)}, f32[96,128]{1,0:T(8,128)S(1)}, u32[]{:S(2)}, u32[]{:S(2)}) collective-permute-start(f32[96,128]{1,0:T(8,128)} %get-tuple-element.14), channel_id=1, source_target_pairs={{0,63},{1,0},{2,1},{3,2},{4,3},{5,4},{6,5},{7,6},{8,7},{9,8},{10,9... | collective-permute-start | bytes 147464 | tf_op jit(solution)/shard_map/ppermute | solution.py:555
  24.2 1.1 %copy-start.2 = (f32[144,8,128]{2,1,0:T(8,128)S(1)}, f32[144,8,128]{2,1,0:T(8,128)}, u32[]{:S(2)}) copy-start(f32[144,8,128]{2,1,0:T(8,128)} %get-tuple-element.11.h_hbm) | copy-start | bytes 1769476
  25.3 0.7 %copy-start.4 = (f32[7,8,128]{2,1,0:T(8,128)S(1)}, f32[7,8,128]{2,1,0:T(8,128)}, u32[]{:S(2)}) copy-start(f32[7,8,128]{2,1,0:T(8,128)} %get-tuple-element.12.s_hbm) | copy-start | bytes 86020
  42.3 10.1 %all-to-all-start.1 = ((f32[4,80,128]{2,1,0:T(8,128)}), f32[4,80,128]{2,1,0:T(8,128)S(1)}, u32[]{:S(2)}, u32[]{:S(2)}) async-start(f32[4,80,128]{2,1,0:T(8,128)} %shard_map.65), calls=%async_computation.1 | async-start | bytes 327680 | tf_op jit(solution)/shard_map/all_to_all | solution.py:576
  46.4 15.9 %collective-permute-start = (f32[600,128]{1,0:T(8,128)S(1)}, f32[600,128]{1,0:T(8,128)S(1)}, u32[]{:S(2)}, u32[]{:S(2)}) collective-permute-start(f32[600,128]{1,0:T(8,128)S(1)} %shard_map.59), channel_id=1, source_target_pairs={{0,63},{1,0},{2,1},{3,2},{4,3},{5,4},{6,5},{7,6},{8,7},{9,8},{10,9... | collective-permute-start | bytes 921608 | tf_op jit(solution)/shard_map/ppermute | solution.py:557
  52.4 9.8 %copy-start.5 = (f32[10]{0:T(128)S(1)}, f32[10]{0:T(128)}, u32[]{:S(2)}) copy-start(f32[10]{0:T(128)} %param.7) | copy-start | bytes 124
  52.5 10.7 %collective-permute-start.2 = (f32[88,128]{1,0:T(8,128)S(1)}, f32[88,128]{1,0:T(8,128)S(1)}, u32[]{:S(2)}, u32[]{:S(2)}) collective-permute-start(f32[88,128]{1,0:T(8,128)S(1)} %get-tuple-element.16), channel_id=1, source_target_pairs={{0,1},{1,2},{2,3},{3,4},{4,5},{5,6},{6,7},{7,8},{8,9},{9,10},{10,1... | collective-permute-start | bytes 135176 | tf_op jit(solution)/shard_map/ppermute | solution.py:583
  54.4 9.6 %collective-permute-start.3 = (f32[88,128]{1,0:T(8,128)S(1)}, f32[88,128]{1,0:T(8,128)S(1)}, u32[]{:S(2)}, u32[]{:S(2)}) collective-permute-start(f32[88,128]{1,0:T(8,128)S(1)} %get-tuple-element.16), channel_id=1, source_target_pairs={{1,0},{2,1},{3,2},{4,3},{5,4},{6,5},{7,6},{8,7},{9,8},{10,9},{11,1... | collective-permute-start | bytes 135176 | tf_op jit(solution)/shard_map/ppermute | solution.py:585

commit v4 on v3

--- a/solution.py
+++ b/solution.py
@@ -508,15 +508,14 @@
     return x.reshape(n, 2, 4, 128).transpose(0, 2, 1, 3).reshape(n, 4, 256)
 
 
-def groups_of(key):
+def stage_groups(space, odd):
     found = {}
     for v in range(16):
-        found.setdefault(key(v), []).append(v)
+        for s in range(space):
+            far = s % 2 == odd
+            key = (v // 8, v % 2) if far else (v % 8 // 2, 2)
+            found.setdefault((key, s), []).append(v * space + s)
     return list(found.values())
-
-
-FAR = groups_of(lambda v: (v // 8, v % 2))
-NEAR = groups_of(lambda v: (v % 8) // 2)
 
 
 def upwind_pairs(space):
@@ -571,9 +570,9 @@
         [pltpu.VMEM((32, 128), F)],
         ins=[SM, VM, VM, VM],
     )
-    got = lax.all_to_all(copies, "vel", 0, 0, axis_index_groups=FAR, tiled=True)
+    got = lax.all_to_all(copies, ("vel", "space"), 0, 0, axis_index_groups=stage_groups(space, 0), tiled=True)
     copies = call(total_kernel, [(4, 80, 128)], [got], 1 << 16, ins=[VM])
-    got = lax.all_to_all(copies, "vel", 0, 0, axis_index_groups=NEAR, tiled=True)
+    got = lax.all_to_all(copies, ("vel", "space"), 0, 0, axis_index_groups=stage_groups(space, 1), tiled=True)
     message, moments_half = call(
         change_kernel, [(88, 128), (80, 128)], [got, old.reshape(80, 128), pore], 1 << 16, ins=[VM] * 3
     )

time: 66.8 us -> 66.7 us (level)
  starting transfers between devices: 38.2 us -> 33.4 us
  waiting for transfers between devices: 0.84 us -> 4.26 us
  blocking collectives: 15.3 us -> 16.6 us
    ppermute x1, starting transfers between devices: 6 us -> 1.92 us  [body(): planes_in = lax.ppermute(planes, ('vel', 'space'), pairs)]
    all_to_all x1, waiting for transfers between devices: 0.01 us -> 3.43 us  [body(): lax.all_to_all(copies, ('vel', 'space'), 0, 0, axis_index_groups=stage_gr...]
    all_to_all x1, blocking collectives: 15.3 us -> 16.6 us  [body(): lax.all_to_all(copies, ('vel', 'space'), 0, 0, axis_index_groups=stage_gr...]
    all_to_all x1, starting transfers between devices: 4.06 us -> 3.36 us  [body(): lax.all_to_all(copies, ('vel', 'space'), 0, 0, axis_index_groups=stage_gr...]
  transfers between devices with their start and end apart: 5 -> 5, of which waited for: 1 -> 2; matrix products, arithmetic and copies ran while one was open for 0% -> 0% of each run, Pallas kernels for 2% -> 2%
where the time goes in v4:
time: 66.7 us; the launch traced here: 66.2 us
  starting transfers between devices  33.4 us (50%)
  blocking collectives  16.6 us (25%)
  Pallas kernels  9.27 us (14%)
  waiting for transfers between devices  4.26 us (6%)
  local copies, waits for them, and re-layouts  1.9 us (3%)
  between operations  0.81 us (1%)
    ppermute x1, starting transfers between devices, body(): sums_in = lax.ppermute(packed, ('vel', 'space'), pairs)  18.3 us
    all_to_all x1, blocking collectives, body(): lax.all_to_all(copies, ('vel', 'space'), 0, 0, axis_index_groups=stage_gr...  16.6 us
    pallas_call x9, Pallas kernels, call(): pl.pallas_call(kernel, out_shape=shapes[0] if single else shapes, in_spec...  9.27 us
    ppermute x1, starting transfers between devices, body(): right = lax.ppermute(message, 'space', [(t, s) for s, t in ring])  7.86 us
    all_to_all x1, waiting for transfers between devices, body(): lax.all_to_all(copies, ('vel', 'space'), 0, 0, axis_index_groups=stage_gr...  3.43 us
    all_to_all x1, starting transfers between devices, body(): lax.all_to_all(copies, ('vel', 'space'), 0, 0, axis_index_groups=stage_gr...  3.36 us
    ppermute x1, starting transfers between devices, body(): planes_in = lax.ppermute(planes, ('vel', 'space'), pairs)  1.92 us
    ppermute x1, starting transfers between devices, body(): left = lax.ppermute(message, 'space', ring)  1.92 us
  transfers between devices with their start and end apart: 5, of which 2 were waited for; matrix products, arithmetic and copies ran while one was open for 0% of the time, Pallas kernels for 2%

profile of v4, /device:TPU:2, one launch (start us, length us, event | category | flops | bytes accessed | tf_op | source)
XLA Modules:
  0.0 66.2 jit_solution(11533678160437054491)
XLA Ops:
  0.6 0.0 copy-start
  0.7 5.1 %shard_map.60 = (f32[96,128]{1,0:T(8,128)}, f32[144,8,128]{2,1,0:T(8,128)}, f32[7,8,128]{2,1,0:T(8,128)}) custom-call(s32[1]{0:T(128)} %bitcast.i_ref, s32[1]{0:T(128)} %bitcast.1.n_ref, f32[1152,128]{1,0:T(8,128)} %bitcast.34, f32[80,128]{1,0:T(8,128)} %bitcast.41, s32[8,128]{1,0:T(8,128)} %bitcast.45), custom_call_target="tpu_custom_call" | custom-call | flops 1048576 | bytes 4194304 | tf_op jit(solution)/shard_map/pallas_call | solution.py:490
  5.8 0.0 copy-start.3
  5.8 18.3 %collective-permute-start.1 = (f32[96,128]{1,0:T(8,128)}, f32[96,128]{1,0:T(8,128)S(1)}, u32[]{:S(2)}, u32[]{:S(2)}) collective-permute-start(f32[96,128]{1,0:T(8,128)} %get-tuple-element.14), channel_id=1, source_target_pairs={{0,63},{1,0},{2,1},{3,2},{4,3},{5,4},{6,5},{7,6},{8,7},{9,8},{10,9... | collective-permute-start | bytes 147464 | tf_op jit(solution)/shard_map/ppermute | solution.py:554
  24.2 0.0 copy-start.2
  24.2 1.1 %copy-done.2 = f32[144,8,128]{2,1,0:T(8,128)S(1)} copy-done((f32[144,8,128]{2,1,0:T(8,128)S(1)}, f32[144,8,128]{2,1,0:T(8,128)}, u32[]{:S(2)}) %copy-start.2) | copy-done | bytes 589848
  25.3 0.7 %copy-done.4 = f32[7,8,128]{2,1,0:T(8,128)S(1)} copy-done((f32[7,8,128]{2,1,0:T(8,128)S(1)}, f32[7,8,128]{2,1,0:T(8,128)}, u32[]{:S(2)}) %copy-start.4) | copy-done | bytes 28696
  26.0 0.2 shard_map.61
  26.2 0.0 collective-permute-done.1.g_ref
  26.2 0.1 shard_map.64
  26.3 16.6 %all_to_all.10.g_ref = f32[4,80,128]{2,1,0:T(8,128)S(1)} all-to-all(f32[4,80,128]{2,1,0:T(8,128)S(1)} %shard_map.64), channel_id=1, replica_groups={{0,128,256,384},{1,65,513,577},{2,130,258,386},{3,67,515,579},{4,132,26..., dimensions={0} | all-to-all | bytes 327680 | tf_op jit(solution)/shard_map/all_to_all | solution.py:573
  42.9 0.7 %shard_map.65 = f32[4,80,128]{2,1,0:T(8,128)} custom-call(f32[4,80,128]{2,1,0:T(8,128)S(1)} %all_to_all.10.g_ref), custom_call_target="tpu_custom_call" | custom-call | flops 65536 | bytes 262144 | tf_op jit(solution)/shard_map/pallas_call | solution.py:490
  43.6 3.4 %all-to-all-start.1 = ((f32[4,80,128]{2,1,0:T(8,128)}), f32[4,80,128]{2,1,0:T(8,128)S(1)}, u32[]{:S(2)}, u32[]{:S(2)}) async-start(f32[4,80,128]{2,1,0:T(8,128)} %shard_map.65), calls=%async_computation.1 | async-start | bytes 327680 | tf_op jit(solution)/shard_map/all_to_all | solution.py:575
  47.0 1.9 %collective-permute-start = (f32[600,128]{1,0:T(8,128)S(1)}, f32[600,128]{1,0:T(8,128)S(1)}, u32[]{:S(2)}, u32[]{:S(2)}) collective-permute-start(f32[600,128]{1,0:T(8,128)S(1)} %shard_map.59), channel_id=1, source_target_pairs={{0,63},{1,0},{2,1},{3,2},{4,3},{5,4},{6,5},{7,6},{8,7},{9,8},{10,9... | collective-permute-start | bytes 921608 | tf_op jit(solution)/shard_map/ppermute | solution.py:556
  48.9 3.4 %all-to-all-done.1.g_ref = f32[4,80,128]{2,1,0:T(8,128)S(1)} async-done(((f32[4,80,128]{2,1,0:T(8,128)}), f32[4,80,128]{2,1,0:T(8,128)S(1)}, u32[]{:S(2)}, u32[]{:S(2)}) %all-to-all-start.1) | async-done | bytes 163872 | tf_op jit(solution)/shard_map/all_to_all | solution.py:575
  52.3 0.0 copy-start.5
  52.3 1.9 %collective-permute-start.2 = (f32[88,128]{1,0:T(8,128)S(1)}, f32[88,128]{1,0:T(8,128)S(1)}, u32[]{:S(2)}, u32[]{:S(2)}) collective-permute-start(f32[88,128]{1,0:T(8,128)S(1)} %get-tuple-element.16), channel_id=1, source_target_pairs={{0,1},{1,2},{2,3},{3,4},{4,5},{5,6},{6,7},{7,8},{8,9},{9,10},{10,1... | collective-permute-start | bytes 135176 | tf_op jit(solution)/shard_map/ppermute | solution.py:582
  54.3 7.9 %collective-permute-start.3 = (f32[88,128]{1,0:T(8,128)S(1)}, f32[88,128]{1,0:T(8,128)S(1)}, u32[]{:S(2)}, u32[]{:S(2)}) collective-permute-start(f32[88,128]{1,0:T(8,128)S(1)} %get-tuple-element.16), channel_id=1, source_target_pairs={{1,0},{2,1},{3,2},{4,3},{5,4},{6,5},{7,6},{8,7},{9,8},{10,9},{11,1... | collective-permute-start | bytes 135176 | tf_op jit(solution)/shard_map/ppermute | solution.py:584
  62.2 0.0 collective-permute-done.refs_0_
  62.2 0.8 %shard_map.62 = f32[1152,128]{1,0:T(8,128)S(1)} custom-call(s32[1]{0:T(128)} %bitcast.i_ref, s32[1]{0:T(128)} %bitcast.1.n_ref, f32[600,128]{1,0:T(8,128)S(1)} %collective-permute-done.refs_0_, s32[8,128]{1,0:T(8,128)S(1)} %bitcast.50, f32[1152,128]{1,0:T(8,128)S(1)} %bitcast.37), custom_call_target="tpu_custom_call" | custom-call | flops 65536 | bytes 262144 | tf_op jit(solution)/shard_map/pallas_call | solution.py:490
  63.0 0.0 collective-permute-done.2
  63.0 0.8 %collective-permute-done.3 = f32[88,128]{1,0:T(8,128)S(1)} collective-permute-done((f32[88,128]{1,0:T(8,128)S(1)}, f32[88,128]{1,0:T(8,128)S(1)}, u32[]{:S(2)}, u32[]{:S(2)}) %collective-permute-start.3) | collective-permute-done | bytes 45088 | tf_op jit(solution)/shard_map/ppermute | solution.py:584
  63.8 0.1 broadcast_in_dim.2.q_ref
  63.9 2.3 %shard_map.67 = (f32[144,8,128]{2,1,0:T(8,128)}, f32[10,8,128]{2,1,0:T(8,128)}) custom-call(s32[1]{0:T(128)} %bitcast.i_ref, s32[1]{0:T(128)} %bitcast.1.n_ref, f32[10,128]{1,0:T(8,128)S(1)} %broadcast_in_dim.2.q_ref, f32[144,8,128]{2,1,0:T(8,128)S(1)} %bitcast.39, f32[144,8,128]{2,1,0:T(8,128)S(1)} %bitcast.40, f32[11,8,128]{2,1,0:T(8,128)S(1)} %bitcast.52, ...), custom_call_target="tpu_custom_call" | custom-call | flops 1048576 | bytes 4194304 | tf_op jit(solution)/shard_map/pallas_call | solution.py:490
  (10 shorter events, 0.1 us)
Async XLA Ops:
  0.6 23.5 %copy-start = (f32[144,4,256]{2,1,0:T(4,128)S(1)}, f32[144,4,256]{2,1,0:T(4,128)}, u32[]{:S(2)}) copy-start(f32[144,4,256]{2,1,0:T(4,128)} %param.4) | copy-start | bytes 1769476
  0.6 23.5 %copy-start.1 = (f32[10,4,256]{2,1,0:T(4,128)S(1)}, f32[10,4,256]{2,1,0:T(4,128)}, u32[]{:S(2)}) copy-start(f32[10,4,256]{2,1,0:T(4,128)} %param.5) | copy-start | bytes 122884
  5.8 18.4 %copy-start.3 = (s32[4,256]{1,0:T(4,128)S(1)}, s32[4,256]{1,0:T(4,128)}, u32[]{:S(2)}) copy-start(s32[4,256]{1,0:T(4,128)} %param.6) | copy-start | bytes 12292
  5.8 20.4 %collective-permute-start.1 = (f32[96,128]{1,0:T(8,128)}, f32[96,128]{1,0:T(8,128)S(1)}, u32[]{:S(2)}, u32[]{:S(2)}) collective-permute-start(f32[96,128]{1,0:T(8,128)} %get-tuple-element.14), channel_id=1, source_target_pairs={{0,63},{1,0},{2,1},{3,2},{4,3},{5,4},{6,5},{7,6},{8,7},{9,8},{10,9... | collective-permute-start | bytes 147464 | tf_op jit(solution)/shard_map/ppermute | solution.py:554
  24.2 1.1 %copy-start.2 = (f32[144,8,128]{2,1,0:T(8,128)S(1)}, f32[144,8,128]{2,1,0:T(8,128)}, u32[]{:S(2)}) copy-start(f32[144,8,128]{2,1,0:T(8,128)} %get-tuple-element.11.h_hbm) | copy-start | bytes 1769476
  25.3 0.7 %copy-start.4 = (f32[7,8,128]{2,1,0:T(8,128)S(1)}, f32[7,8,128]{2,1,0:T(8,128)}, u32[]{:S(2)}) copy-start(f32[7,8,128]{2,1,0:T(8,128)} %get-tuple-element.12.s_hbm) | copy-start | bytes 86020
  43.6 8.7 %all-to-all-start.1 = ((f32[4,80,128]{2,1,0:T(8,128)}), f32[4,80,128]{2,1,0:T(8,128)S(1)}, u32[]{:S(2)}, u32[]{:S(2)}) async-start(f32[4,80,128]{2,1,0:T(8,128)} %shard_map.65), calls=%async_computation.1 | async-start | bytes 327680 | tf_op jit(solution)/shard_map/all_to_all | solution.py:575
  47.0 15.2 %collective-permute-start = (f32[600,128]{1,0:T(8,128)S(1)}, f32[600,128]{1,0:T(8,128)S(1)}, u32[]{:S(2)}, u32[]{:S(2)}) collective-permute-start(f32[600,128]{1,0:T(8,128)S(1)} %shard_map.59), channel_id=1, source_target_pairs={{0,63},{1,0},{2,1},{3,2},{4,3},{5,4},{6,5},{7,6},{8,7},{9,8},{10,9... | collective-permute-start | bytes 921608 | tf_op jit(solution)/shard_map/ppermute | solution.py:556
  52.3 9.8 %copy-start.5 = (f32[10]{0:T(128)S(1)}, f32[10]{0:T(128)}, u32[]{:S(2)}) copy-start(f32[10]{0:T(128)} %param.7) | copy-start | bytes 124
  52.3 10.7 %collective-permute-start.2 = (f32[88,128]{1,0:T(8,128)S(1)}, f32[88,128]{1,0:T(8,128)S(1)}, u32[]{:S(2)}, u32[]{:S(2)}) collective-permute-start(f32[88,128]{1,0:T(8,128)S(1)} %get-tuple-element.16), channel_id=1, source_target_pairs={{0,1},{1,2},{2,3},{3,4},{4,5},{5,6},{6,7},{7,8},{8,9},{9,10},{10,1... | collective-permute-start | bytes 135176 | tf_op jit(solution)/shard_map/ppermute | solution.py:582
  54.3 9.6 %collective-permute-start.3 = (f32[88,128]{1,0:T(8,128)S(1)}, f32[88,128]{1,0:T(8,128)S(1)}, u32[]{:S(2)}, u32[]{:S(2)}) collective-permute-start(f32[88,128]{1,0:T(8,128)S(1)} %get-tuple-element.16), channel_id=1, source_target_pairs={{1,0},{2,1},{3,2},{4,3},{5,4},{6,5},{7,6},{8,7},{9,8},{10,9},{11,1... | collective-permute-start | bytes 135176 | tf_op jit(solution)/shard_map/ppermute | solution.py:584

commit v5 on v4

--- a/solution.py
+++ b/solution.py
@@ -87,7 +87,7 @@
     )
 
 
-def sums_kernel(i_ref, n_ref, x_hbm, m_hbm, p_hbm, g_ref, h_hbm, s_hbm, x_ref, m_ref, p_ref, h_ref, s_ref, sem):
+def sums_kernel(i_ref, n_ref, x_hbm, m_hbm, p_hbm, g_ref, h_hbm, s_hbm, x_ref, m_ref, p_ref, h_ref, s_ref, w_ref, sem):
     def rows_of(j):
         rows = pl.ds(96 * j, 96)
         return pltpu.make_async_copy(x_hbm.at[rows], x_ref.at[rows], sem.at[2 + j])
@@ -106,7 +106,15 @@
     even_row = (sub & 1) == 0
     zero = jnp.zeros(SHAPE, F)
     cs = [-2.75 + 0.5 * (4 * t + (sub >> 1)).astype(F) for t in range(3)]
-    ecs = [jnp.exp(-c * c) for c in cs]
+    ecs = [jnp.exp(-c * c - a * a) for c in cs]
+    top, first = sub < 4, (sub & 2) == 0
+    for jj in range(6):
+        bm = magnitude(jj)
+        for t in range(3):
+            ca = jnp.abs(cs[t])
+            r = 1.0 / (aa + ca + (1.0 + bm))
+            for n, x in enumerate((aa * r, bm * r, ca * r, (math.exp(-bm * bm) * ecs[t]) * r, aa * r * r)):
+                w_ref[(3 * jj + t) * 5 + n] = x
     for copy in copies:
         copy.wait()
 
@@ -128,21 +136,23 @@
         pore = pair(p_ref, near)
         al = field_polynomial(a, [pair(m_ref, 8 * m + near) for m in range(10)])
 
+        def packed(x):
+            y = [
+                jnp.where(top, x[n], x[n + 2]) + pltpu.roll(jnp.where(top, x[n + 2], x[n]), 4, 0) for n in range(2)
+            ]
+            return jnp.where(first, y[0], y[1]) + jnp.where(first, pltpu.roll(y[0], 6, 0), pltpu.roll(y[1], 2, 0))
+
         def step(jj, carry):
-            whole, down, up, minus, plus, double = carry
+            below, above, minus, plus, whole = carry
             rows_of(jj).wait()
             rows_of(11 - jj).wait()
             bm = 2.75 - 0.5 * jj.astype(F)
-            ex = jnp.exp(-(a * a) - bm * bm)
             polys = [at_second(al, -bm), at_second(al, bm)]
             outs = [[zero] * 4, [zero] * 4]
-            powers = [[[zero] * 5] * 3, [[zero] * 5] * 3]
+            powers = [[], []]
             for t in range(3):
                 c = cs[t]
-                ca = jnp.abs(c)
-                r = 1.0 / (aa + ca + (1.0 + bm))
-                wa, wb, wc = aa * r, bm * r, ca * r
-                rg = r * ex * ecs[t]
+                wa, wb, wc, rg, wr = [w_ref[(3 * jj + t) * 5 + n] for n in range(5)]
                 for side in range(2):
                     p0, p1, p2, p3 = polys[side]
                     g = rg * (p0 + c * (p1 + c * (p2 + c * p3)))
@@ -151,34 +161,53 @@
                     h = (wa * pore) * (
                         g + wa * f2 + wb * from_y(f1, lane, side == 1, swap_pairs) + wc * back(f1, t)
                     )
-                    k = wa * r * f1
-                    ks, hs = [k], [h]
+                    ks, hs = [wr * f1], [h]
                     for _ in range(4):
                         ks.append(c * ks[-1])
                     for _ in range(3):
                         hs.append(c * hs[-1])
-                    powers[side] = powers[side][:t] + [ks] + powers[side][t + 1 :]
+                    powers[side].append(ks)
                     outs[side] = [p + q for p, q in zip(outs[side], hs)]
-            sides = [down, up]
+            b2 = bm * bm
+            b3, b4 = b2 * bm, b2 * b2
+            sides = [below, above]
+            parts = []
             for side in range(2):
-                b = bm if side else -bm
                 low, mid, high = powers[side]
-                total = [low[n] + mid[n] + high[n] for n in range(4)]
-                sides[side] = add_raw(sides[side], b, [bm * x for x in total])
-                double = add_raw(double, b, total)
-                minus = add_raw(minus, b, [low[n] + jnp.where(sub < 4, mid[n], 0.0) for n in range(1, 5)])
-                plus = add_raw(plus, b, [high[n] + jnp.where(sub < 4, 0.0, mid[n]) for n in range(1, 5)])
-                whole = add_raw(whole, b, outs[side])
-            return whole, sides[0], sides[1], minus, plus, double
-
-        groups = lax.fori_loop(0, 6, step, ((zero,) * 7,) * 6)
-        scale = (1.0, 1.0, 1.0, -1.0, 1.0, aa)
+                total = packed([low[n] + mid[n] + high[n] for n in range(4)])
+                parts.append(
+                    (
+                        packed([low[n] + jnp.where(sub < 4, mid[n], 0.0) for n in range(1, 5)]),
+                        packed([high[n] + jnp.where(sub < 4, 0.0, mid[n]) for n in range(1, 5)]),
+                        packed(outs[side]),
+                    )
+                )
+                sides[side] = [x + y * total for x, y in zip(sides[side], (1.0, bm, b2, b3, b4))]
+
+            def both(acc, n):
+                even, odd = parts[1][n] + parts[0][n], parts[1][n] - parts[0][n]
+                return [acc[0] + even, acc[1] + bm * odd, acc[2] + b2 * even, acc[3] + b3 * odd]
+
+            return sides[0], sides[1], both(minus, 0), both(plus, 1), both(whole, 2)
+
+        below, above, minus, plus, whole = lax.fori_loop(
+            0, 6, step, ([zero] * 5, [zero] * 5, [zero] * 4, [zero] * 4, [zero] * 4)
+        )
+        signs = (1.0, -1.0, 1.0, -1.0)
+        groups = (
+            whole,
+            [signs[n] * below[n + 1] for n in range(4)],
+            above[1:],
+            [-x for x in minus],
+            plus,
+            [aa * (above[n] + signs[n] * below[n]) for n in range(4)],
+        )
         for n in range(6):
-            for m in range(7):
-                x = groups[n][m]
-                x = x + pltpu.roll(x, 2, 0)
-                x = (x + pltpu.roll(x, 4, 0)) * scale[n]
-                g_ref[16 * n + 2 * m : 16 * n + 2 * m + 2, :] = x[0:2, :]
+            t0, t1, t2, t3 = groups[n]
+            g_ref[16 * n : 16 * n + 4, :] = t0[0:4, :]
+            g_ref[16 * n + 4 : 16 * n + 8, :] = t1[0:4, :]
+            g_ref[16 * n + 8 : 16 * n + 12, :] = (t2 + pltpu.roll(t0, 4, 0))[0:4, :]
+            g_ref[16 * n + 12 : 16 * n + 14, :] = (t3 + pltpu.roll(t1, 4, 0))[0:2, :]
             g_ref[16 * n + 14 : 16 * n + 16, :] = jnp.zeros((2, 128), F)
 
     pl.when(i_ref[0] >= 8)(lambda: build(3, 2))
@@ -315,8 +344,8 @@
         return jnp.where(sub < 4, row(e_ref, r), row(e_ref, r + 1))
 
     s0, sb, sc, s2, sb2, sc2, sbc = [
-        s_ref[n] + jnp.where(at_near, spread(2 * n), jnp.where(at_far, spread(16 + 2 * n), 0.0))
-        for n in range(7)
+        s_ref[n] + jnp.where(at_near, spread(r), jnp.where(at_far, spread(16 + r), 0.0))
+        for n, r in enumerate((0, 4, 2, 8, 12, 10, 6))
     ]
     a2 = a * a
     t4, t5 = (a2 - 1.5) * s0 + s2, (a2 - 2.5) * s0 + s2
@@ -544,6 +573,7 @@
             pltpu.VMEM((8, 128), jnp.int32),
             pltpu.VMEM((144, 8, 128), F),
             pltpu.VMEM((7, 8, 128), F),
+            pltpu.VMEM((90, 8, 128), F),
             pltpu.SemaphoreType.DMA((14,)),
         ],
         [SM, SM, HBM, HBM, HBM],

time: 66.7 us -> 66.7 us (level)
  no operation moved by 1% of the time
where the time goes in v5:
time: 66.7 us; the launch traced here: 66.2 us
  starting transfers between devices  33.4 us (50%)
  blocking collectives  16.6 us (25%)
  Pallas kernels  9.26 us (14%)
  waiting for transfers between devices  4.26 us (6%)
  local copies, waits for them, and re-layouts  1.9 us (3%)
  between operations  0.81 us (1%)
    ppermute x1, starting transfers between devices, body(): sums_in = lax.ppermute(packed, ('vel', 'space'), pairs)  18.3 us
    all_to_all x1, blocking collectives, body(): lax.all_to_all(copies, ('vel', 'space'), 0, 0, axis_index_groups=stage_gr...  16.6 us
    pallas_call x9, Pallas kernels, call(): pl.pallas_call(kernel, out_shape=shapes[0] if single else shapes, in_spec...  9.26 us
    ppermute x1, starting transfers between devices, body(): right = lax.ppermute(message, 'space', [(t, s) for s, t in ring])  7.86 us
    all_to_all x1, waiting for transfers between devices, body(): lax.all_to_all(copies, ('vel', 'space'), 0, 0, axis_index_groups=stage_gr...  3.43 us
    all_to_all x1, starting transfers between devices, body(): lax.all_to_all(copies, ('vel', 'space'), 0, 0, axis_index_groups=stage_gr...  3.36 us
    ppermute x1, starting transfers between devices, body(): planes_in = lax.ppermute(planes, ('vel', 'space'), pairs)  1.92 us
    ppermute x1, starting transfers between devices, body(): left = lax.ppermute(message, 'space', ring)  1.92 us
  transfers between devices with their start and end apart: 5, of which 2 were waited for; matrix products, arithmetic and copies ran while one was open for 0% of the time, Pallas kernels for 2%

profile of v5, /device:TPU:2, one launch (start us, length us, event | category | flops | bytes accessed | tf_op | source)
XLA Modules:
  0.0 66.2 jit_solution(17057304625838054270)
XLA Ops:
  0.7 5.1 %shard_map.60 = (f32[96,128]{1,0:T(8,128)}, f32[144,8,128]{2,1,0:T(8,128)}, f32[7,8,128]{2,1,0:T(8,128)}) custom-call(s32[1]{0:T(128)} %bitcast.i_ref, s32[1]{0:T(128)} %bitcast.1.n_ref, f32[1152,128]{1,0:T(8,128)} %bitcast.34, f32[80,128]{1,0:T(8,128)} %bitcast.41, s32[8,128]{1,0:T(8,128)} %bitcast.45), custom_call_target="tpu_custom_call" | custom-call | flops 1048576 | bytes 4194304 | tf_op jit(solution)/shard_map/pallas_call | solution.py:519
  5.8 0.0 copy-start.3
  5.8 18.3 %collective-permute-start.1 = (f32[96,128]{1,0:T(8,128)}, f32[96,128]{1,0:T(8,128)S(1)}, u32[]{:S(2)}, u32[]{:S(2)}) collective-permute-start(f32[96,128]{1,0:T(8,128)} %get-tuple-element.14), channel_id=1, source_target_pairs={{0,63},{1,0},{2,1},{3,2},{4,3},{5,4},{6,5},{7,6},{8,7},{9,8},{10,9... | collective-permute-start | bytes 147464 | tf_op jit(solution)/shard_map/ppermute | solution.py:584
  24.2 0.0 copy-done
  24.2 0.0 copy-start.2
  24.2 1.1 %copy-done.2 = f32[144,8,128]{2,1,0:T(8,128)S(1)} copy-done((f32[144,8,128]{2,1,0:T(8,128)S(1)}, f32[144,8,128]{2,1,0:T(8,128)}, u32[]{:S(2)}) %copy-start.2) | copy-done | bytes 589848
  25.3 0.7 %copy-done.4 = f32[7,8,128]{2,1,0:T(8,128)S(1)} copy-done((f32[7,8,128]{2,1,0:T(8,128)S(1)}, f32[7,8,128]{2,1,0:T(8,128)}, u32[]{:S(2)}) %copy-start.4) | copy-done | bytes 28696
  26.0 0.2 shard_map.61
  26.2 0.0 collective-permute-done.1.g_ref
  26.2 0.1 shard_map.64
  26.3 16.6 %all_to_all.10.g_ref = f32[4,80,128]{2,1,0:T(8,128)S(1)} all-to-all(f32[4,80,128]{2,1,0:T(8,128)S(1)} %shard_map.64), channel_id=1, replica_groups={{0,128,256,384},{1,65,513,577},{2,130,258,386},{3,67,515,579},{4,132,26..., dimensions={0} | all-to-all | bytes 327680 | tf_op jit(solution)/shard_map/all_to_all | solution.py:603
  42.9 0.7 %shard_map.65 = f32[4,80,128]{2,1,0:T(8,128)} custom-call(f32[4,80,128]{2,1,0:T(8,128)S(1)} %all_to_all.10.g_ref), custom_call_target="tpu_custom_call" | custom-call | flops 65536 | bytes 262144 | tf_op jit(solution)/shard_map/pallas_call | solution.py:519
  43.6 3.4 %all-to-all-start.1 = ((f32[4,80,128]{2,1,0:T(8,128)}), f32[4,80,128]{2,1,0:T(8,128)S(1)}, u32[]{:S(2)}, u32[]{:S(2)}) async-start(f32[4,80,128]{2,1,0:T(8,128)} %shard_map.65), calls=%async_computation.1 | async-start | bytes 327680 | tf_op jit(solution)/shard_map/all_to_all | solution.py:605
  47.0 1.9 %collective-permute-start = (f32[600,128]{1,0:T(8,128)S(1)}, f32[600,128]{1,0:T(8,128)S(1)}, u32[]{:S(2)}, u32[]{:S(2)}) collective-permute-start(f32[600,128]{1,0:T(8,128)S(1)} %shard_map.59), channel_id=1, source_target_pairs={{0,63},{1,0},{2,1},{3,2},{4,3},{5,4},{6,5},{7,6},{8,7},{9,8},{10,9... | collective-permute-start | bytes 921608 | tf_op jit(solution)/shard_map/ppermute | solution.py:586
  48.9 3.4 %all-to-all-done.1.g_ref = f32[4,80,128]{2,1,0:T(8,128)S(1)} async-done(((f32[4,80,128]{2,1,0:T(8,128)}), f32[4,80,128]{2,1,0:T(8,128)S(1)}, u32[]{:S(2)}, u32[]{:S(2)}) %all-to-all-start.1) | async-done | bytes 163872 | tf_op jit(solution)/shard_map/all_to_all | solution.py:605
  52.3 0.0 copy-start.5
  52.3 1.9 %collective-permute-start.2 = (f32[88,128]{1,0:T(8,128)S(1)}, f32[88,128]{1,0:T(8,128)S(1)}, u32[]{:S(2)}, u32[]{:S(2)}) collective-permute-start(f32[88,128]{1,0:T(8,128)S(1)} %get-tuple-element.16), channel_id=1, source_target_pairs={{0,1},{1,2},{2,3},{3,4},{4,5},{5,6},{6,7},{7,8},{8,9},{9,10},{10,1... | collective-permute-start | bytes 135176 | tf_op jit(solution)/shard_map/ppermute | solution.py:612
  54.3 7.9 %collective-permute-start.3 = (f32[88,128]{1,0:T(8,128)S(1)}, f32[88,128]{1,0:T(8,128)S(1)}, u32[]{:S(2)}, u32[]{:S(2)}) collective-permute-start(f32[88,128]{1,0:T(8,128)S(1)} %get-tuple-element.16), channel_id=1, source_target_pairs={{1,0},{2,1},{3,2},{4,3},{5,4},{6,5},{7,6},{8,7},{9,8},{10,9},{11,1... | collective-permute-start | bytes 135176 | tf_op jit(solution)/shard_map/ppermute | solution.py:614
  62.2 0.0 collective-permute-done.refs_0_
  62.2 0.8 %shard_map.62 = f32[1152,128]{1,0:T(8,128)S(1)} custom-call(s32[1]{0:T(128)} %bitcast.i_ref, s32[1]{0:T(128)} %bitcast.1.n_ref, f32[600,128]{1,0:T(8,128)S(1)} %collective-permute-done.refs_0_, s32[8,128]{1,0:T(8,128)S(1)} %bitcast.50, f32[1152,128]{1,0:T(8,128)S(1)} %bitcast.37), custom_call_target="tpu_custom_call" | custom-call | flops 65536 | bytes 262144 | tf_op jit(solution)/shard_map/pallas_call | solution.py:519
  63.0 0.0 collective-permute-done.2
  63.0 0.8 %collective-permute-done.3 = f32[88,128]{1,0:T(8,128)S(1)} collective-permute-done((f32[88,128]{1,0:T(8,128)S(1)}, f32[88,128]{1,0:T(8,128)S(1)}, u32[]{:S(2)}, u32[]{:S(2)}) %collective-permute-start.3) | collective-permute-done | bytes 45088 | tf_op jit(solution)/shard_map/ppermute | solution.py:614
  63.8 0.1 broadcast_in_dim.2.q_ref
  63.9 2.3 %shard_map.67 = (f32[144,8,128]{2,1,0:T(8,128)}, f32[10,8,128]{2,1,0:T(8,128)}) custom-call(s32[1]{0:T(128)} %bitcast.i_ref, s32[1]{0:T(128)} %bitcast.1.n_ref, f32[10,128]{1,0:T(8,128)S(1)} %broadcast_in_dim.2.q_ref, f32[144,8,128]{2,1,0:T(8,128)S(1)} %bitcast.39, f32[144,8,128]{2,1,0:T(8,128)S(1)} %bitcast.40, f32[11,8,128]{2,1,0:T(8,128)S(1)} %bitcast.52, ...), custom_call_target="tpu_custom_call" | custom-call | flops 1048576 | bytes 4194304 | tf_op jit(solution)/shard_map/pallas_call | solution.py:519
  (10 shorter events, 0.1 us)
Async XLA Ops:
  0.6 23.5 %copy-start = (f32[144,4,256]{2,1,0:T(4,128)S(1)}, f32[144,4,256]{2,1,0:T(4,128)}, u32[]{:S(2)}) copy-start(f32[144,4,256]{2,1,0:T(4,128)} %param.4) | copy-start | bytes 1769476
  0.6 23.5 %copy-start.1 = (f32[10,4,256]{2,1,0:T(4,128)S(1)}, f32[10,4,256]{2,1,0:T(4,128)}, u32[]{:S(2)}) copy-start(f32[10,4,256]{2,1,0:T(4,128)} %param.5) | copy-start | bytes 122884
  5.8 18.4 %copy-start.3 = (s32[4,256]{1,0:T(4,128)S(1)}, s32[4,256]{1,0:T(4,128)}, u32[]{:S(2)}) copy-start(s32[4,256]{1,0:T(4,128)} %param.6) | copy-start | bytes 12292
  5.8 20.4 %collective-permute-start.1 = (f32[96,128]{1,0:T(8,128)}, f32[96,128]{1,0:T(8,128)S(1)}, u32[]{:S(2)}, u32[]{:S(2)}) collective-permute-start(f32[96,128]{1,0:T(8,128)} %get-tuple-element.14), channel_id=1, source_target_pairs={{0,63},{1,0},{2,1},{3,2},{4,3},{5,4},{6,5},{7,6},{8,7},{9,8},{10,9... | collective-permute-start | bytes 147464 | tf_op jit(solution)/shard_map/ppermute | solution.py:584
  24.2 1.1 %copy-start.2 = (f32[144,8,128]{2,1,0:T(8,128)S(1)}, f32[144,8,128]{2,1,0:T(8,128)}, u32[]{:S(2)}) copy-start(f32[144,8,128]{2,1,0:T(8,128)} %get-tuple-element.11.h_hbm) | copy-start | bytes 1769476
  25.3 0.7 %copy-start.4 = (f32[7,8,128]{2,1,0:T(8,128)S(1)}, f32[7,8,128]{2,1,0:T(8,128)}, u32[]{:S(2)}) copy-start(f32[7,8,128]{2,1,0:T(8,128)} %get-tuple-element.12.s_hbm) | copy-start | bytes 86020
  43.6 8.7 %all-to-all-start.1 = ((f32[4,80,128]{2,1,0:T(8,128)}), f32[4,80,128]{2,1,0:T(8,128)S(1)}, u32[]{:S(2)}, u32[]{:S(2)}) async-start(f32[4,80,128]{2,1,0:T(8,128)} %shard_map.65), calls=%async_computation.1 | async-start | bytes 327680 | tf_op jit(solution)/shard_map/all_to_all | solution.py:605
  47.0 15.2 %collective-permute-start = (f32[600,128]{1,0:T(8,128)S(1)}, f32[600,128]{1,0:T(8,128)S(1)}, u32[]{:S(2)}, u32[]{:S(2)}) collective-permute-start(f32[600,128]{1,0:T(8,128)S(1)} %shard_map.59), channel_id=1, source_target_pairs={{0,63},{1,0},{2,1},{3,2},{4,3},{5,4},{6,5},{7,6},{8,7},{9,8},{10,9... | collective-permute-start | bytes 921608 | tf_op jit(solution)/shard_map/ppermute | solution.py:586
  52.3 9.8 %copy-start.5 = (f32[10]{0:T(128)S(1)}, f32[10]{0:T(128)}, u32[]{:S(2)}) copy-start(f32[10]{0:T(128)} %param.7) | copy-start | bytes 124
  52.3 10.7 %collective-permute-start.2 = (f32[88,128]{1,0:T(8,128)S(1)}, f32[88,128]{1,0:T(8,128)S(1)}, u32[]{:S(2)}, u32[]{:S(2)}) collective-permute-start(f32[88,128]{1,0:T(8,128)S(1)} %get-tuple-element.16), channel_id=1, source_target_pairs={{0,1},{1,2},{2,3},{3,4},{4,5},{5,6},{6,7},{7,8},{8,9},{9,10},{10,1... | collective-permute-start | bytes 135176 | tf_op jit(solution)/shard_map/ppermute | solution.py:612
  54.3 9.6 %collective-permute-start.3 = (f32[88,128]{1,0:T(8,128)S(1)}, f32[88,128]{1,0:T(8,128)S(1)}, u32[]{:S(2)}, u32[]{:S(2)}) collective-permute-start(f32[88,128]{1,0:T(8,128)S(1)} %get-tuple-element.16), channel_id=1, source_target_pairs={{1,0},{2,1},{3,2},{4,3},{5,4},{6,5},{7,6},{8,7},{9,8},{10,9},{11,1... | collective-permute-start | bytes 135176 | tf_op jit(solution)/shard_map/ppermute | solution.py:614

commit v6 on v5

--- a/solution.py
+++ b/solution.py
@@ -436,7 +436,7 @@
     pl.when(i_ref[0] < 8)(lambda: fix(3, 2))
 
 
-def final_kernel(i_ref, n_ref, q_ref, e_ref, l_ref, c_ref, left_ref, right_ref, mh_ref, o_hbm, mo_ref, k_ref, o_ref, sem):
+def final_kernel(i_ref, n_ref, q_ref, e_ref, l_ref, c_ref, left_ref, right_ref, mh_ref, o_hbm, mo_hbm, k_ref, mo_ref, o_ref, sem):
     a = first_speed(i_ref)
     sub, lane = iotas()
     pores = [left_ref[10], c_ref[10], right_ref[10]]
@@ -473,6 +473,8 @@
         k_ref[m] = cor[1]
         mo_ref[m] = mh_ref[m] + cor[1]
 
+    moments_out = pltpu.make_async_copy(mo_ref, mo_hbm, sem.at[12])
+    moments_out.start()
     al = field_polynomial(a, [k_ref[m] for m in range(10)])
     pore = pores[1]
 
@@ -505,6 +507,7 @@
     for jj in range(6):
         chunk(jj, jj).wait()
         chunk(6 + jj, 11 - jj).wait()
+    moments_out.wait()
 
 
 VM = pl.BlockSpec(memory_space=pltpu.VMEM)
@@ -629,9 +632,14 @@
             moments_half.reshape(10, 8, 128),
         ],
         1 << 20,
-        [pltpu.VMEM((10, 8, 128), F), pltpu.VMEM((144, 8, 128), F), pltpu.SemaphoreType.DMA((12,))],
+        [
+            pltpu.VMEM((10, 8, 128), F),
+            pltpu.VMEM((10, 8, 128), F),
+            pltpu.VMEM((144, 8, 128), F),
+            pltpu.SemaphoreType.DMA((13,)),
+        ],
         [SM, SM] + [VM] * 7,
-        [HBM, VM],
+        [HBM, HBM],
     )
     return from_registers(out), from_registers(moments_new)
 

time: 66.7 us -> 66.1 us (level)
  no operation moved by 1% of the time
where the time goes in v6:
time: 66.1 us; the launch traced here: 65.6 us
  starting transfers between devices  33.4 us (51%)
  blocking collectives  16.6 us (25%)
  Pallas kernels  8.66 us (13%)
  waiting for transfers between devices  4.26 us (6%)
  local copies, waits for them, and re-layouts  1.9 us (3%)
  between operations  0.81 us (1%)
    ppermute x1, starting transfers between devices, body(): sums_in = lax.ppermute(packed, ('vel', 'space'), pairs)  18.3 us
    all_to_all x1, blocking collectives, body(): lax.all_to_all(copies, ('vel', 'space'), 0, 0, axis_index_groups=stage_gr...  16.6 us
    pallas_call x9, Pallas kernels, call(): pl.pallas_call(kernel, out_shape=shapes[0] if single else shapes, in_spec...  8.66 us
    ppermute x1, starting transfers between devices, body(): right = lax.ppermute(message, 'space', [(t, s) for s, t in ring])  7.86 us
    all_to_all x1, waiting for transfers between devices, body(): lax.all_to_all(copies, ('vel', 'space'), 0, 0, axis_index_groups=stage_gr...  3.43 us
    all_to_all x1, starting transfers between devices, body(): lax.all_to_all(copies, ('vel', 'space'), 0, 0, axis_index_groups=stage_gr...  3.36 us
    ppermute x1, starting transfers between devices, body(): planes_in = lax.ppermute(planes, ('vel', 'space'), pairs)  1.92 us
    ppermute x1, starting transfers between devices, body(): left = lax.ppermute(message, 'space', ring)  1.92 us
  transfers between devices with their start and end apart: 5, of which 2 were waited for; matrix products, arithmetic and copies ran while one was open for 0% of the time, Pallas kernels for 2%

profile of v6, /device:TPU:2, one launch (start us, length us, event | category | flops | bytes accessed | tf_op | source)
XLA Modules:
  0.0 65.6 jit_solution(3806815625079470298)
XLA Ops:
  0.7 5.1 %shard_map.60 = (f32[96,128]{1,0:T(8,128)}, f32[144,8,128]{2,1,0:T(8,128)}, f32[7,8,128]{2,1,0:T(8,128)}) custom-call(s32[1]{0:T(128)} %bitcast.i_ref, s32[1]{0:T(128)} %bitcast.1.n_ref, f32[1152,128]{1,0:T(8,128)} %bitcast.34, f32[80,128]{1,0:T(8,128)} %bitcast.41, s32[8,128]{1,0:T(8,128)} %bitcast.45), custom_call_target="tpu_custom_call" | custom-call | flops 1048576 | bytes 4194304 | tf_op jit(solution)/shard_map/pallas_call | solution.py:522
  5.8 0.0 copy-start.3
  5.8 18.3 %collective-permute-start.1 = (f32[96,128]{1,0:T(8,128)}, f32[96,128]{1,0:T(8,128)S(1)}, u32[]{:S(2)}, u32[]{:S(2)}) collective-permute-start(f32[96,128]{1,0:T(8,128)} %get-tuple-element.14), channel_id=1, source_target_pairs={{0,63},{1,0},{2,1},{3,2},{4,3},{5,4},{6,5},{7,6},{8,7},{9,8},{10,9... | collective-permute-start | bytes 147464 | tf_op jit(solution)/shard_map/ppermute | solution.py:587
  24.2 0.0 copy-done
  24.2 0.0 copy-start.2
  24.2 1.1 %copy-done.2 = f32[144,8,128]{2,1,0:T(8,128)S(1)} copy-done((f32[144,8,128]{2,1,0:T(8,128)S(1)}, f32[144,8,128]{2,1,0:T(8,128)}, u32[]{:S(2)}) %copy-start.2) | copy-done | bytes 589848
  25.3 0.7 %copy-done.4 = f32[7,8,128]{2,1,0:T(8,128)S(1)} copy-done((f32[7,8,128]{2,1,0:T(8,128)S(1)}, f32[7,8,128]{2,1,0:T(8,128)}, u32[]{:S(2)}) %copy-start.4) | copy-done | bytes 28696
  26.0 0.2 shard_map.61
  26.2 0.0 collective-permute-done.1.g_ref
  26.2 0.1 shard_map.64
  26.3 16.6 %all_to_all.10.g_ref = f32[4,80,128]{2,1,0:T(8,128)S(1)} all-to-all(f32[4,80,128]{2,1,0:T(8,128)S(1)} %shard_map.64), channel_id=1, replica_groups={{0,128,256,384},{1,65,513,577},{2,130,258,386},{3,67,515,579},{4,132,26..., dimensions={0} | all-to-all | bytes 327680 | tf_op jit(solution)/shard_map/all_to_all | solution.py:606
  42.9 0.7 %shard_map.65 = f32[4,80,128]{2,1,0:T(8,128)} custom-call(f32[4,80,128]{2,1,0:T(8,128)S(1)} %all_to_all.10.g_ref), custom_call_target="tpu_custom_call" | custom-call | flops 65536 | bytes 262144 | tf_op jit(solution)/shard_map/pallas_call | solution.py:522
  43.6 3.4 %all-to-all-start.1 = ((f32[4,80,128]{2,1,0:T(8,128)}), f32[4,80,128]{2,1,0:T(8,128)S(1)}, u32[]{:S(2)}, u32[]{:S(2)}) async-start(f32[4,80,128]{2,1,0:T(8,128)} %shard_map.65), calls=%async_computation.1 | async-start | bytes 327680 | tf_op jit(solution)/shard_map/all_to_all | solution.py:608
  47.0 1.9 %collective-permute-start = (f32[600,128]{1,0:T(8,128)S(1)}, f32[600,128]{1,0:T(8,128)S(1)}, u32[]{:S(2)}, u32[]{:S(2)}) collective-permute-start(f32[600,128]{1,0:T(8,128)S(1)} %shard_map.59), channel_id=1, source_target_pairs={{0,63},{1,0},{2,1},{3,2},{4,3},{5,4},{6,5},{7,6},{8,7},{9,8},{10,9... | collective-permute-start | bytes 921608 | tf_op jit(solution)/shard_map/ppermute | solution.py:589
  48.9 3.4 %all-to-all-done.1.g_ref = f32[4,80,128]{2,1,0:T(8,128)S(1)} async-done(((f32[4,80,128]{2,1,0:T(8,128)}), f32[4,80,128]{2,1,0:T(8,128)S(1)}, u32[]{:S(2)}, u32[]{:S(2)}) %all-to-all-start.1) | async-done | bytes 163872 | tf_op jit(solution)/shard_map/all_to_all | solution.py:608
  52.3 0.0 copy-start.5
  52.3 1.9 %collective-permute-start.2 = (f32[88,128]{1,0:T(8,128)S(1)}, f32[88,128]{1,0:T(8,128)S(1)}, u32[]{:S(2)}, u32[]{:S(2)}) collective-permute-start(f32[88,128]{1,0:T(8,128)S(1)} %get-tuple-element.16), channel_id=1, source_target_pairs={{0,1},{1,2},{2,3},{3,4},{4,5},{5,6},{6,7},{7,8},{8,9},{9,10},{10,1... | collective-permute-start | bytes 135176 | tf_op jit(solution)/shard_map/ppermute | solution.py:615
  54.3 7.9 %collective-permute-start.3 = (f32[88,128]{1,0:T(8,128)S(1)}, f32[88,128]{1,0:T(8,128)S(1)}, u32[]{:S(2)}, u32[]{:S(2)}) collective-permute-start(f32[88,128]{1,0:T(8,128)S(1)} %get-tuple-element.16), channel_id=1, source_target_pairs={{1,0},{2,1},{3,2},{4,3},{5,4},{6,5},{7,6},{8,7},{9,8},{10,9},{11,1... | collective-permute-start | bytes 135176 | tf_op jit(solution)/shard_map/ppermute | solution.py:617
  62.2 0.0 collective-permute-done.refs_0_
  62.2 0.8 %shard_map.62 = f32[1152,128]{1,0:T(8,128)S(1)} custom-call(s32[1]{0:T(128)} %bitcast.i_ref, s32[1]{0:T(128)} %bitcast.1.n_ref, f32[600,128]{1,0:T(8,128)S(1)} %collective-permute-done.refs_0_, s32[8,128]{1,0:T(8,128)S(1)} %bitcast.50, f32[1152,128]{1,0:T(8,128)S(1)} %bitcast.37), custom_call_target="tpu_custom_call" | custom-call | flops 65536 | bytes 262144 | tf_op jit(solution)/shard_map/pallas_call | solution.py:522
  63.0 0.0 collective-permute-done.2
  63.0 0.8 %collective-permute-done.3 = f32[88,128]{1,0:T(8,128)S(1)} collective-permute-done((f32[88,128]{1,0:T(8,128)S(1)}, f32[88,128]{1,0:T(8,128)S(1)}, u32[]{:S(2)}, u32[]{:S(2)}) %collective-permute-start.3) | collective-permute-done | bytes 45088 | tf_op jit(solution)/shard_map/ppermute | solution.py:617
  63.8 0.1 broadcast_in_dim.2.q_ref
  63.9 1.7 %shard_map.67 = (f32[144,8,128]{2,1,0:T(8,128)}, f32[10,8,128]{2,1,0:T(8,128)}) custom-call(s32[1]{0:T(128)} %bitcast.i_ref, s32[1]{0:T(128)} %bitcast.1.n_ref, f32[10,128]{1,0:T(8,128)S(1)} %broadcast_in_dim.2.q_ref, f32[144,8,128]{2,1,0:T(8,128)S(1)} %bitcast.39, f32[144,8,128]{2,1,0:T(8,128)S(1)} %bitcast.40, f32[11,8,128]{2,1,0:T(8,128)S(1)} %bitcast.52, ...), custom_call_target="tpu_custom_call" | custom-call | flops 1048576 | bytes 4194304 | tf_op jit(solution)/shard_map/pallas_call | solution.py:522
  (10 shorter events, 0.1 us)
Async XLA Ops:
  0.6 23.5 %copy-start = (f32[144,4,256]{2,1,0:T(4,128)S(1)}, f32[144,4,256]{2,1,0:T(4,128)}, u32[]{:S(2)}) copy-start(f32[144,4,256]{2,1,0:T(4,128)} %param.4) | copy-start | bytes 1769476
  0.6 23.5 %copy-start.1 = (f32[10,4,256]{2,1,0:T(4,128)S(1)}, f32[10,4,256]{2,1,0:T(4,128)}, u32[]{:S(2)}) copy-start(f32[10,4,256]{2,1,0:T(4,128)} %param.5) | copy-start | bytes 122884
  5.8 18.4 %copy-start.3 = (s32[4,256]{1,0:T(4,128)S(1)}, s32[4,256]{1,0:T(4,128)}, u32[]{:S(2)}) copy-start(s32[4,256]{1,0:T(4,128)} %param.6) | copy-start | bytes 12292
  5.8 20.4 %collective-permute-start.1 = (f32[96,128]{1,0:T(8,128)}, f32[96,128]{1,0:T(8,128)S(1)}, u32[]{:S(2)}, u32[]{:S(2)}) collective-permute-start(f32[96,128]{1,0:T(8,128)} %get-tuple-element.14), channel_id=1, source_target_pairs={{0,63},{1,0},{2,1},{3,2},{4,3},{5,4},{6,5},{7,6},{8,7},{9,8},{10,9... | collective-permute-start | bytes 147464 | tf_op jit(solution)/shard_map/ppermute | solution.py:587
  24.2 1.1 %copy-start.2 = (f32[144,8,128]{2,1,0:T(8,128)S(1)}, f32[144,8,128]{2,1,0:T(8,128)}, u32[]{:S(2)}) copy-start(f32[144,8,128]{2,1,0:T(8,128)} %get-tuple-element.11.h_hbm) | copy-start | bytes 1769476
  25.3 0.7 %copy-start.4 = (f32[7,8,128]{2,1,0:T(8,128)S(1)}, f32[7,8,128]{2,1,0:T(8,128)}, u32[]{:S(2)}) copy-start(f32[7,8,128]{2,1,0:T(8,128)} %get-tuple-element.12.s_hbm) | copy-start | bytes 86020
  43.6 8.7 %all-to-all-start.1 = ((f32[4,80,128]{2,1,0:T(8,128)}), f32[4,80,128]{2,1,0:T(8,128)S(1)}, u32[]{:S(2)}, u32[]{:S(2)}) async-start(f32[4,80,128]{2,1,0:T(8,128)} %shard_map.65), calls=%async_computation.1 | async-start | bytes 327680 | tf_op jit(solution)/shard_map/all_to_all | solution.py:608
  47.0 15.2 %collective-permute-start = (f32[600,128]{1,0:T(8,128)S(1)}, f32[600,128]{1,0:T(8,128)S(1)}, u32[]{:S(2)}, u32[]{:S(2)}) collective-permute-start(f32[600,128]{1,0:T(8,128)S(1)} %shard_map.59), channel_id=1, source_target_pairs={{0,63},{1,0},{2,1},{3,2},{4,3},{5,4},{6,5},{7,6},{8,7},{9,8},{10,9... | collective-permute-start | bytes 921608 | tf_op jit(solution)/shard_map/ppermute | solution.py:589
  52.3 9.8 %copy-start.5 = (f32[10]{0:T(128)S(1)}, f32[10]{0:T(128)}, u32[]{:S(2)}) copy-start(f32[10]{0:T(128)} %param.7) | copy-start | bytes 124
  52.3 10.7 %collective-permute-start.2 = (f32[88,128]{1,0:T(8,128)S(1)}, f32[88,128]{1,0:T(8,128)S(1)}, u32[]{:S(2)}, u32[]{:S(2)}) collective-permute-start(f32[88,128]{1,0:T(8,128)S(1)} %get-tuple-element.16), channel_id=1, source_target_pairs={{0,1},{1,2},{2,3},{3,4},{4,5},{5,6},{6,7},{7,8},{8,9},{9,10},{10,1... | collective-permute-start | bytes 135176 | tf_op jit(solution)/shard_map/ppermute | solution.py:615
  54.3 9.6 %collective-permute-start.3 = (f32[88,128]{1,0:T(8,128)S(1)}, f32[88,128]{1,0:T(8,128)S(1)}, u32[]{:S(2)}, u32[]{:S(2)}) collective-permute-start(f32[88,128]{1,0:T(8,128)S(1)} %get-tuple-element.16), channel_id=1, source_target_pairs={{1,0},{2,1},{3,2},{4,3},{5,4},{6,5},{7,6},{8,7},{9,8},{10,9},{11,1... | collective-permute-start | bytes 135176 | tf_op jit(solution)/shard_map/ppermute | solution.py:617
